TPU v7x, 32 devices: a whole 2x2x4 slice. The times are simulated.
32 devices in a mesh: dp: 8 (over z, core), tensor: 4 (over y, x).
Axes of the slice: x: 2, y: 2, z: 4, core: 2. Of those that a mesh axis runs over, the one named last changes fastest.
Arguments:
- tokens: bfloat16 [8192, 2048], P(('dp', 'tensor')), may hold values from -6 to 6
- lengths: int32 [8], P('dp'), may hold values from 512 to 1024, as said below
- routes: int32 [8192, 4], P(('dp', 'tensor')), may hold values from 0 to 7, all different within a row; in each aligned block of 256 rows (0 to 255, 256 to 511, ...) at most 192 rows name the same one
- attn_gain: float32 [2048], replicated, may hold values from 0.5 to 1.5
- w_query: bfloat16 [2048, 2048], P('dp', 'tensor')
- w_key: bfloat16 [2048, 2048], P('dp', 'tensor'), may hold values from -0.125 to 0.125
- w_value: bfloat16 [2048, 2048], P('dp', 'tensor'), may hold values from -0.125 to 0.125
- w_output: bfloat16 [2048, 2048], P('tensor', 'dp'), may hold values from -0.5 to 0.5
- moe_gain: float32 [2048], replicated, may hold values from 0.5 to 1.5
- w_router: float32 [2048, 8], replicated, may hold values from -0.0625 to 0.0625
- w_sigmoid: float32 [2048], replicated, may hold values from -0.125 to 0.125
- shared_gate: bfloat16 [2048, 5632], P('dp', 'tensor'), may hold values from -0.125 to 0.125
- shared_up: bfloat16 [2048, 5632], P('dp', 'tensor'), may hold values from -0.125 to 0.125
- shared_down: bfloat16 [5632, 2048], P('tensor', 'dp'), may hold values from -0.15625 to 0.15625
- expert_gate: bfloat16 [8, 2048, 1408], P('dp', 'tensor'), may hold values from -0.125 to 0.125
- expert_up: bfloat16 [8, 2048, 1408], P('dp', 'tensor'), may hold values from -0.125 to 0.125
- expert_down: bfloat16 [8, 1408, 2048], P('dp', None, 'tensor'), may hold values from -0.3125 to 0.3125
- cotangent: bfloat16 [8192, 2048], P(('dp', 'tensor')), may hold values from -6 to 6
Outputs:
- block_out: bfloat16 [8192, 2048], P(('dp', 'tensor'))
- d_tokens: float32 [8192, 2048], P(('dp', 'tensor'))
- d_attn_gain: float32 [2048], replicated
- d_w_query: float32 [2048, 2048], P('dp', 'tensor')
- d_w_key: float32 [2048, 2048], P('dp', 'tensor')
- d_w_value: float32 [2048, 2048], P('dp', 'tensor')
- d_w_output: float32 [2048, 2048], P('tensor', 'dp')
- d_moe_gain: float32 [2048], replicated
- d_w_router: float32 [2048, 8], replicated
- d_w_sigmoid: float32 [2048], replicated
- d_shared_gate: float32 [2048, 5632], P('dp', 'tensor')
- d_shared_up: float32 [2048, 5632], P('dp', 'tensor')
- d_shared_down: float32 [5632, 2048], P('tensor', 'dp')
- d_expert_gate: float32 [8, 2048, 1408], P('dp', 'tensor')
- d_expert_up: float32 [8, 2048, 1408], P('dp', 'tensor')
- d_expert_down: float32 [8, 1408, 2048], P('dp', None, 'tensor')
- clip_scale: float32 [16], P('tensor')
- query_clipped: bfloat16 [2048, 2048], P('dp', 'tensor')
- key_clipped: bfloat16 [2048, 2048], P('dp', 'tensor')
Inputs may be any that keep to these rules, and one draw needn't show every extreme that they name: Positions from lengths[s] to 1023 of sequence s are padding; the first sequence has none. Among the rows of one device no expert is named by more than 192 routes.
All inputs are finite; a program needn't handle non-finite values.
Results may differ from a plain program's by a relative error of at most 0.024.
Values may be sent and summed in bfloat16 or wider, within the bound.
No kernel may reach another device: no remote copies, remote signals or barrier semaphores. Data moves between devices by JAX's collectives and lax.ppermute only.
A program may use at most 320 MiB of HBM per device.

v0:
```python
import jax
import jax.numpy as jnp
from jax import lax
from jax.sharding import PartitionSpec as P

DH = 128


EPS = 1e-06
CLIP_LIMIT = 6.0
NEG = -1e30
HIGH = lax.Precision.HIGHEST
CONTRACT_LAST = (((1,), (1,)), ((), ()))
CONTRACT_FIRST = (((0,), (0,)), ((), ()))


def norm_rows(inputs, gain):
    factor = lax.rsqrt(jnp.mean(inputs * inputs, axis=-1, keepdims=True) + EPS)
    return (inputs * factor * gain, factor)


def norm_back(inputs, factor, gain, upstream):
    scaled = upstream * gain
    inner = jnp.mean(scaled * inputs, axis=-1, keepdims=True)
    return (
        factor * scaled - inputs * (factor * factor * factor) * inner,
        jnp.sum(upstream * inputs * factor, axis=0),
    )


def silu_slope(values_in):
    sigma = jax.nn.sigmoid(values_in)
    return sigma * (1.0 + values_in * (1.0 - sigma))


def group_rows(local_rows):
    return lax.all_gather(local_rows, "tensor", axis=0, tiled=True)


def split_rows(partial_sum):
    return lax.psum_scatter(
        partial_sum.astype(jnp.bfloat16), "tensor", scatter_dimension=0, tiled=True
    ).astype(jnp.float32)


def trade_slots(slot_rows):
    return lax.all_to_all(slot_rows, "dp", split_axis=0, concat_axis=0, tiled=True)


def project_in(gathered, weight):
    return jnp.dot(
        gathered,
        lax.all_gather(weight, "dp", axis=0, tiled=True),
        preferred_element_type=jnp.float32,
    )


def project_out(hidden, weight):
    return jnp.dot(
        hidden, lax.all_gather(weight, "dp", axis=1, tiled=True), preferred_element_type=jnp.float32
    )


def back_through_in(grad_cols, weight):
    return lax.dot_general(
        grad_cols,
        lax.all_gather(weight, "dp", axis=0, tiled=True),
        CONTRACT_LAST,
        preferred_element_type=jnp.float32,
    )


def back_through_out(grad_rows, weight):
    return lax.dot_general(
        grad_rows,
        lax.all_gather(weight, "dp", axis=1, tiled=True),
        CONTRACT_LAST,
        preferred_element_type=jnp.float32,
    )


def grads_in(gathered, grad_cols):
    return lax.psum_scatter(
        lax.dot_general(
            gathered, grad_cols, CONTRACT_FIRST, preferred_element_type=jnp.float32
        ).astype(jnp.bfloat16),
        "dp",
        scatter_dimension=0,
        tiled=True,
    ).astype(jnp.float32)


def grads_out(hidden, grad_rows):
    product = lax.dot_general(hidden, grad_rows, CONTRACT_FIRST, preferred_element_type=jnp.float32)
    return lax.psum_scatter(
        product.astype(jnp.bfloat16), "dp", scatter_dimension=1, tiled=True
    ).astype(jnp.float32)


def attention_forward(queries, keys_in, values_in, length, factor):
    seq_len = queries.shape[0]
    block_len = min(512, seq_len)
    position = jnp.arange(seq_len, dtype=jnp.int32)

    def one_block(offset):
        rows_here = offset + jnp.arange(block_len, dtype=jnp.int32)
        query_block = lax.dynamic_slice_in_dim(queries, offset, block_len, 0)
        allowed = (position[None, :] <= rows_here[:, None]) & (position[None, :] < length)
        raw_scores = (
            jnp.einsum("qhd,khd->hqk", query_block, keys_in, preferred_element_type=jnp.float32)
            * factor
        )
        scores = jnp.where(allowed[None], raw_scores, NEG)
        highest = jnp.max(scores, axis=2, keepdims=True)
        log_total = highest + jnp.log(jnp.sum(jnp.exp(scores - highest), axis=2, keepdims=True))
        weights = jnp.exp(scores - log_total).astype(jnp.bfloat16)
        attended = jnp.einsum(
            "hqk,khd->qhd", weights, values_in, preferred_element_type=jnp.float32
        )
        counted = allowed & (rows_here[:, None] < length)
        peak_here = jnp.max(jnp.where(counted[None], raw_scores, NEG), axis=(1, 2))
        return (attended.astype(jnp.bfloat16), log_total[:, :, 0], peak_here)

    offsets = jnp.arange(seq_len // block_len, dtype=jnp.int32) * block_len
    attended, log_totals, peaks = lax.map(one_block, offsets)
    return (attended.reshape(seq_len, -1), log_totals, jnp.max(peaks, axis=0))


def attention_backward(queries, keys_in, values_in, grad_out, log_totals, length, factor):
    seq_len = queries.shape[0]
    block_len = log_totals.shape[2]
    position = jnp.arange(seq_len, dtype=jnp.int32)

    def one_block(sums, packed):
        key_sum, value_sum = sums
        offset, log_total = packed
        rows_here = offset + jnp.arange(block_len, dtype=jnp.int32)
        query_block = lax.dynamic_slice_in_dim(queries, offset, block_len, 0)
        grad_block = lax.dynamic_slice_in_dim(grad_out, offset, block_len, 0)
        allowed = (position[None, :] <= rows_here[:, None]) & (position[None, :] < length)
        raw_scores = (
            jnp.einsum("qhd,khd->hqk", query_block, keys_in, preferred_element_type=jnp.float32)
            * factor
        )
        scores = jnp.where(allowed[None], raw_scores, NEG)
        probs = jnp.exp(scores - log_total[:, :, None])
        weights = probs.astype(jnp.bfloat16)
        along = jnp.einsum(
            "qhd,khd->hqk", grad_block, values_in, preferred_element_type=jnp.float32
        )
        inner = jnp.sum(probs * along, axis=2, keepdims=True)
        grad_scores = (probs * (along - inner)).astype(jnp.bfloat16)
        grad_query = (
            jnp.einsum("hqk,khd->qhd", grad_scores, keys_in, preferred_element_type=jnp.float32)
            * factor
        )
        key_sum = (
            key_sum
            + jnp.einsum(
                "hqk,qhd->khd", grad_scores, query_block, preferred_element_type=jnp.float32
            )
            * factor
        )
        value_sum = value_sum + jnp.einsum(
            "hqk,qhd->khd", weights, grad_block, preferred_element_type=jnp.float32
        )
        return ((key_sum, value_sum), grad_query.astype(jnp.bfloat16))

    offsets = jnp.arange(seq_len // block_len, dtype=jnp.int32) * block_len
    start_zero = jnp.zeros(keys_in.shape, jnp.float32)
    (key_sum, value_sum), grad_query = lax.scan(
        one_block, (start_zero, start_zero), (offsets, log_totals)
    )
    return (
        grad_query.reshape(seq_len, -1),
        key_sum.astype(jnp.bfloat16).reshape(seq_len, -1),
        value_sum.astype(jnp.bfloat16).reshape(seq_len, -1),
    )


def local(
    tokens,
    lengths,
    routes,
    attn_gain,
    w_query,
    w_key,
    w_value,
    w_output,
    moe_gain,
    w_router,
    w_sigmoid,
    shared_gate,
    shared_up,
    shared_down,
    expert_gate,
    expert_up,
    expert_down,
    cotangent,
):
    factor = DH ** (-0.5)
    inputs = tokens.astype(jnp.float32)
    normed, inv_one = norm_rows(inputs, attn_gain)
    gathered_one = group_rows(normed.astype(jnp.bfloat16))
    seq_len = gathered_one.shape[0]
    width = w_query.shape[1]
    in_weights = jnp.concatenate([w_query, w_key, w_value], axis=1)
    projected = project_in(gathered_one, in_weights).astype(jnp.bfloat16)
    queries = projected[:, :width].reshape(seq_len, -1, DH)
    keys_in = projected[:, width : 2 * width].reshape(seq_len, -1, DH)
    values_in = projected[:, 2 * width :].reshape(seq_len, -1, DH)
    length = lengths[0]
    attended, log_totals, peaks = attention_forward(queries, keys_in, values_in, length, factor)
    peaks = lax.pmax(peaks, "dp")
    middle = inputs + split_rows(project_out(attended, w_output))
    moe_norm, inv_two = norm_rows(middle, moe_gain)
    moe_low = moe_norm.astype(jnp.bfloat16)
    moe_wide = moe_low.astype(jnp.float32)
    experts = w_router.shape[1]
    rows_dev, route_count = routes.shape
    model_width = tokens.shape[1]
    capacity = rows_dev * route_count * 3 // (2 * experts)
    logits = jnp.dot(moe_wide, w_router, precision=HIGH)
    picked = (routes[:, :, None] == jnp.arange(experts, dtype=jnp.int32)[None, None, :]).astype(
        jnp.float32
    )
    chosen = jnp.sum(picked * logits[:, None, :], axis=2)
    gates = jax.nn.softmax(chosen, axis=1)
    flat_routes = routes.reshape(-1)
    onehot = (flat_routes[:, None] == jnp.arange(experts, dtype=jnp.int32)[None, :]).astype(
        jnp.int32
    )
    placed = jnp.sum((jnp.cumsum(onehot, axis=0) - onehot) * onehot, axis=1)
    flat_slot = flat_routes * capacity + placed
    pair_count = rows_dev * route_count
    slot_owner = (
        jnp.full((experts * capacity,), pair_count, jnp.int32)
        .at[flat_slot]
        .set(jnp.arange(pair_count, dtype=jnp.int32))
    )
    padded = jnp.concatenate([moe_low, jnp.zeros((1, model_width), jnp.bfloat16)], axis=0)
    owned = trade_slots(
        padded[slot_owner // route_count].reshape(experts, capacity, model_width)
    ).reshape(-1, model_width)
    fetched = (
        lax.all_gather(expert_gate, "tensor", axis=1, tiled=True),
        lax.all_gather(expert_up, "tensor", axis=1, tiled=True),
        lax.all_gather(expert_down, "tensor", axis=2, tiled=True),
    )
    full_gate, full_up, full_down = (fetched[0][0], fetched[1][0], fetched[2][0])
    gate_pre = jnp.dot(owned, full_gate, preferred_element_type=jnp.float32)
    up_pre = jnp.dot(owned, full_up, preferred_element_type=jnp.float32)
    expert_hidden = (jax.nn.silu(gate_pre) * up_pre).astype(jnp.bfloat16)
    expert_result = jnp.dot(expert_hidden, full_down, preferred_element_type=jnp.float32).astype(
        jnp.bfloat16
    )
    returned = trade_slots(expert_result.reshape(experts, capacity, model_width)).reshape(
        -1, model_width
    )
    pair_out = returned[flat_slot].reshape(rows_dev, route_count, model_width).astype(jnp.float32)
    routed = jnp.sum(gates[:, :, None] * pair_out, axis=1)
    gathered_two = group_rows(moe_low)
    shared_in = jnp.concatenate([shared_gate, shared_up], axis=1)
    hidden_width = shared_gate.shape[1]
    shared_pre = project_in(gathered_two, shared_in)
    shared_act = jax.nn.silu(shared_pre[:, :hidden_width])
    shared_hidden = (shared_act * shared_pre[:, hidden_width:]).astype(jnp.bfloat16)
    shared_rows = split_rows(project_out(shared_hidden, shared_down))
    mixing = jax.nn.sigmoid(jnp.dot(moe_wide, w_sigmoid, precision=HIGH))
    combined = middle + routed + mixing[:, None] * shared_rows
    upstream = cotangent.astype(jnp.float32)
    d_shared_rows = (mixing[:, None] * upstream).astype(jnp.bfloat16)
    d_mixing = mixing * (1.0 - mixing) * jnp.sum(shared_rows * upstream, axis=1)
    whole_shared = group_rows(d_shared_rows)
    d_shared_down = grads_out(shared_hidden, whole_shared)
    d_hidden = back_through_out(whole_shared, shared_down)
    d_gate_shared = (
        d_hidden * shared_pre[:, hidden_width:] * silu_slope(shared_pre[:, :hidden_width])
    )
    d_up_shared = d_hidden * shared_act
    d_shared_pre = jnp.concatenate([d_gate_shared, d_up_shared], axis=1).astype(jnp.bfloat16)
    d_shared_in = grads_in(gathered_two, d_shared_pre)
    d_from_shared = split_rows(back_through_in(d_shared_pre, shared_in))
    d_pairs = (
        (gates[:, :, None] * upstream[:, None, :]).astype(jnp.bfloat16).reshape(-1, model_width)
    )
    d_gates = jnp.sum(pair_out * upstream[:, None, :], axis=2)
    d_chosen = gates * (d_gates - jnp.sum(gates * d_gates, axis=1, keepdims=True))
    d_logits = jnp.sum(picked * d_chosen[:, :, None], axis=1)
    padded_grad = jnp.concatenate([d_pairs, jnp.zeros((1, model_width), jnp.bfloat16)], axis=0)
    owned_grad = trade_slots(
        padded_grad[slot_owner].reshape(experts, capacity, model_width)
    ).reshape(-1, model_width)
    refetched = (
        lax.all_gather(expert_gate, "tensor", axis=1, tiled=True),
        lax.all_gather(expert_up, "tensor", axis=1, tiled=True),
        lax.all_gather(expert_down, "tensor", axis=2, tiled=True),
    )
    back_gate, back_up, back_down = (refetched[0][0], refetched[1][0], refetched[2][0])
    d_expert_hidden = lax.dot_general(
        owned_grad, back_down, CONTRACT_LAST, preferred_element_type=jnp.float32
    )
    d_down_full = lax.dot_general(
        expert_hidden, owned_grad, CONTRACT_FIRST, preferred_element_type=jnp.float32
    )
    d_gate_expert = (d_expert_hidden * up_pre * silu_slope(gate_pre)).astype(jnp.bfloat16)
    d_up_expert = (d_expert_hidden * jax.nn.silu(gate_pre)).astype(jnp.bfloat16)
    d_gate_full = lax.dot_general(
        owned, d_gate_expert, CONTRACT_FIRST, preferred_element_type=jnp.float32
    )
    d_up_full = lax.dot_general(
        owned, d_up_expert, CONTRACT_FIRST, preferred_element_type=jnp.float32
    )
    d_owned = (
        lax.dot_general(d_gate_expert, back_gate, CONTRACT_LAST, preferred_element_type=jnp.float32)
        + lax.dot_general(d_up_expert, back_up, CONTRACT_LAST, preferred_element_type=jnp.float32)
    ).astype(jnp.bfloat16)
    d_returned = trade_slots(d_owned.reshape(experts, capacity, model_width)).reshape(
        -1, model_width
    )
    d_from_routed = jnp.sum(
        d_returned[flat_slot].reshape(rows_dev, route_count, model_width).astype(jnp.float32),
        axis=1,
    )
    expert_sums = (
        lax.psum_scatter(
            d_gate_full.astype(jnp.bfloat16), "tensor", scatter_dimension=0, tiled=True
        ).astype(jnp.float32),
        lax.psum_scatter(
            d_up_full.astype(jnp.bfloat16), "tensor", scatter_dimension=0, tiled=True
        ).astype(jnp.float32),
        lax.psum_scatter(
            d_down_full.astype(jnp.bfloat16), "tensor", scatter_dimension=1, tiled=True
        ).astype(jnp.float32),
    )
    d_moe = (
        d_from_shared
        + d_from_routed
        + jnp.dot(d_logits, w_router.T, precision=HIGH)
        + d_mixing[:, None] * w_sigmoid[None, :]
    )
    d_router_part = jnp.dot(moe_wide.T, d_logits, precision=HIGH)
    d_sigmoid_part = jnp.dot(d_mixing, moe_wide, precision=HIGH)
    d_middle_norm, d_moe_gain_part = norm_back(middle, inv_two, moe_gain, d_moe)
    d_middle = upstream + d_middle_norm
    whole_middle = group_rows(d_middle.astype(jnp.bfloat16))
    d_w_output = grads_out(attended, whole_middle)
    d_attended = (
        back_through_out(whole_middle, w_output).astype(jnp.bfloat16).reshape(seq_len, -1, DH)
    )
    d_queries, d_keys, d_values = attention_backward(
        queries, keys_in, values_in, d_attended, log_totals, length, factor
    )
    d_projected = jnp.concatenate([d_queries, d_keys, d_values], axis=1)
    d_in_weights = grads_in(gathered_one, d_projected)
    d_normed = split_rows(back_through_in(d_projected, in_weights))
    d_inputs_norm, d_attn_gain_part = norm_back(inputs, inv_one, attn_gain, d_normed)
    d_tokens = d_middle + d_inputs_norm
    small_sums = lax.psum(
        (d_attn_gain_part, d_moe_gain_part, d_router_part, d_sigmoid_part), ("dp", "tensor")
    )
    clip_scale = jnp.sqrt(CLIP_LIMIT / jnp.maximum(peaks, CLIP_LIMIT))
    columns = jnp.repeat(clip_scale, DH)
    query_clipped = (w_query.astype(jnp.float32) * columns[None, :]).astype(jnp.bfloat16)
    key_clipped = (w_key.astype(jnp.float32) * columns[None, :]).astype(jnp.bfloat16)
    return (
        combined.astype(jnp.bfloat16),
        d_tokens,
        small_sums[0],
        d_in_weights[:, :width],
        d_in_weights[:, width : 2 * width],
        d_in_weights[:, 2 * width :],
        d_w_output,
        small_sums[1],
        small_sums[2],
        small_sums[3],
        d_shared_in[:, :hidden_width],
        d_shared_in[:, hidden_width:],
        d_shared_down,
        expert_sums[0][None],
        expert_sums[1][None],
        expert_sums[2][None],
        clip_scale,
        query_clipped,
        key_clipped,
    )


def solution(mesh):
    placed = (
        P(("dp", "tensor"), None),
        P("dp"),
        P(("dp", "tensor"), None),
        P(),
        P("dp", "tensor"),
        P("dp", "tensor"),
        P("dp", "tensor"),
        P("tensor", "dp"),
        P(),
        P(),
        P(),
        P("dp", "tensor"),
        P("dp", "tensor"),
        P("tensor", "dp"),
        P("dp", "tensor", None),
        P("dp", "tensor", None),
        P("dp", None, "tensor"),
        P(("dp", "tensor"), None),
    )
    return jax.shard_map(
        local,
        mesh=mesh,
        in_specs=placed,
        out_specs=(
            P(("dp", "tensor"), None),
            P(("dp", "tensor"), None),
            P(),
            P("dp", "tensor"),
            P("dp", "tensor"),
            P("dp", "tensor"),
            P("tensor", "dp"),
            P(),
            P(),
            P(),
            P("dp", "tensor"),
            P("dp", "tensor"),
            P("tensor", "dp"),
            P("dp", "tensor", None),
            P("dp", "tensor", None),
            P("dp", None, "tensor"),
            P("tensor"),
            P("dp", "tensor"),
            P("dp", "tensor"),
        ),
        check_vma=False,
    )
```

profile of v0, /device:TPU:0, one launch (start us, length us, event | category | flops | bytes accessed | tf_op | source)
XLA Modules:
  0.0 1984.3 jit_solution(1717854227678014054)
XLA Ops:
  14.4 53.6 %all-gather.12.cloned.1.call-done = bf16[1024,2048]{1,0:T(8,128)(2,1)} async-done(((bf16[256,2048]{1,0:T(8,128)(2,1)}), bf16[1024,2048]{1,0:T(8,128)(2,1)}) %all-gather.12.cloned.1.call-update) | async-done | bytes 4194320 | tf_op jit(solution)/shard_map/all_gather | solution.py:37
  68.0 66.9 %all-gather.14.cloned.1.call-done = bf16[2048,1536]{1,0:T(8,128)(2,1)} async-done(((bf16[256,1536]{1,0:T(8,128)(2,1)}), bf16[2048,1536]{1,0:T(8,128)(2,1)}) %all-gather.14.cloned.1.call-update) | async-done | bytes 6291472 | tf_op jit(solution)/shard_map/all_gather | solution.py:53
  147.3 32.9 %while.32 = (s32[]{:T(128)}, bf16[2,512,4,128]{3,2,1,0:T(4,128)(2,1)}, f32[2,4,512]{2,1,0:T(4,128)S(1)}, f32[2,4]{1,0:T(2,128)S(1)}, s32[2]{0:T(128)S(1)}, /*ind...) while((s32[]{:T(128)}, ...), condition=%wide.region_5.6_spmd.clone.clone, body=%wide.region_1.5_spmd.clone.clone.sunk | while | flops 1102840320 | bytes 40967468 | solution.py:125
  190.3 48.9 %reduce-scatter.12.cloned.1.call-done = bf16[256,2048]{1,0:T(8,128)(2,1)} async-done(((bf16[1024,2048]{1,0:T(8,128)(2,1)}), bf16[256,2048]{1,0:T(8,128)(2,1)}) %reduce-scatter.12.cloned.1.call-update) | async-done | bytes 1048592 | tf_op jit(solution)/shard_map/reduce_scatter | solution.py:41
  307.1 175.1 %all-to-all-done = bf16[8,192,2048]{2,1,0:T(8,128)(2,1)} async-done(((bf16[8,192,2048]{2,1,0:T(8,128)(2,1)}), bf16[8,192,2048]{2,1,0:T(8,128)(2,1)}, u32[]{:S(2)}, u32[]{:S(2)}) %all-to-all-start) | async-done | bytes 6291488 | tf_op jit(solution)/shard_map/all_to_all | solution.py:47
  487.4 20.6 %all-gather.24.cloned.1.call-done = bf16[1024,2048]{1,0:T(8,128)(2,1)} async-done(((bf16[256,2048]{1,0:T(8,128)(2,1)}), bf16[1024,2048]{1,0:T(8,128)(2,1)}) %all-gather.24.cloned.1.call-update) | async-done | bytes 4194320 | tf_op jit(solution)/shard_map/all_gather | solution.py:37
  508.0 17.2 fusion.89
  531.2 118.1 %all-gather.28.cloned.1.call-done = bf16[1408,2048]{1,0:T(8,128)(2,1)} async-done(((bf16[1408,256]{1,0:T(8,128)(2,1)}), bf16[1408,2048]{1,0:T(8,128)(2,1)}) %all-gather.28.cloned.1.call-update) | async-done | bytes 5767184 | tf_op jit(solution)/shard_map/all_gather | solution.py:60
  660.2 54.9 %all-gather.20.cloned.1.call-done = bf16[1,2048,1408]{2,1,0:T(8,128)(2,1)} async-done(((bf16[1,512,1408]{2,1,0:T(8,128)(2,1)}), bf16[1,2048,1408]{2,1,0:T(8,128)(2,1)}) %all-gather.20.cloned.1.call-update) | async-done | bytes 5767184 | tf_op jit(solution)/shard_map/all_gather | solution.py:247
  730.1 52.5 %all-gather.18.cloned.1.call-done = bf16[1,2048,1408]{2,1,0:T(8,128)(2,1)} async-done(((bf16[1,512,1408]{2,1,0:T(8,128)(2,1)}), bf16[1,2048,1408]{2,1,0:T(8,128)(2,1)}) %all-gather.18.cloned.1.call-update) | async-done | bytes 5767184 | tf_op jit(solution)/shard_map/all_gather | solution.py:246
  797.8 52.1 %all-gather.22.cloned.1.call-done = bf16[1,1408,2048]{2,1,0:T(8,128)(2,1)} async-done(((bf16[1,1408,512]{2,1,0:T(8,128)(2,1)}), bf16[1,1408,2048]{2,1,0:T(8,128)(2,1)}) %all-gather.22.cloned.1.call-update) | async-done | bytes 5767184 | tf_op jit(solution)/shard_map/all_gather | solution.py:248
  849.8 23.0 %multiply_convert_fusion.1 = (bf16[1536,1408]{1,0:T(8,128)(2,1)}, bf16[1536,1408]{1,0:T(8,128)(2,1)}, bf16[1536,1408]{1,0:T(8,128)(2,1)}) fusion(f32[1536,1408]{1,0:T(8,128)} %fusion.48, f32[1536,1408]{1,0:T(8,128)} %fusion.44, bf16[1536,2048]{1,0:T(8,128)(2,1)} %bitcast.14, bf16[1,1408,2048]{2,1,0:T(8,128)(2,1)} %all-gather.22.cloned.1.call-done), kind=kOutput, calls=%fused_computation.64 | convolution fusion | flops 8890810368 | bytes 42336256 | tf_op jit(solution)/shard_map/dot_general | solution.py:300
  930.0 119.8 %all-to-all-done.3 = bf16[8,192,2048]{2,1,0:T(8,128)(2,1)} async-done(((bf16[8,192,2048]{2,1,0:T(8,128)(2,1)}), bf16[8,192,2048]{2,1,0:T(8,128)(2,1)}, u32[]{:S(2)}, u32[]{:S(2)}) %all-to-all-start.3) | async-done | bytes 6291488 | tf_op jit(solution)/shard_map/all_to_all | solution.py:47
  1110.8 82.7 %all-to-all-done.1 = bf16[8,192,2048]{2,1,0:T(8,128)(2,1)} async-done(((bf16[8,192,2048]{2,1,0:T(8,128)(2,1)}), bf16[8,192,2048]{2,1,0:T(8,128)(2,1)}, u32[]{:S(2)}, u32[]{:S(2)}) %all-to-all-start.1) | async-done | bytes 6291488 | tf_op jit(solution)/shard_map/all_to_all | solution.py:47
  1318.3 52.5 %while.33 = (s32[]{:T(128)}, f32[1024,4,128]{0,2,1:T(8,128)S(1)}, f32[1024,4,128]{0,2,1:T(8,128)}, bf16[2,512,4,128]{3,2,1,0:T(4,128)(2,1)}, s32[2]{0:T(128)S(1)...) while((s32[]{:T(128)}, f32[1024,4,128]{0,2,1:T(8,128)S(1)}, ...), condition=%wide.region_26.27_spmd.clone.clone, body=%wide.region_24.26_spmd.clone.clone.sunk | while | flops 2720005632 | bytes 189332000 | solution.py:171
  1387.9 18.5 convolution_convert_fusion
  1443.2 57.6 %reduce-scatter.28.cloned.1.call-done = bf16[512,1408]{1,0:T(8,128)(2,1)} async-done(((bf16[2048,1408]{1,0:T(8,128)(2,1)}), bf16[512,1408]{1,0:T(8,128)(2,1)}) %reduce-scatter.28.cloned.1.call-update) | async-done | bytes 1441808 | tf_op jit(solution)/shard_map/reduce_scatter | solution.py:326
  1504.0 63.8 %reduce-scatter.26.cloned.1.call-done = bf16[1408,256]{1,0:T(8,128)(2,1)} async-done(((bf16[1408,2048]{1,0:T(8,128)(2,1)}), bf16[1408,256]{1,0:T(8,128)(2,1)}) %reduce-scatter.26.cloned.1.call-update) | async-done | bytes 720912 | tf_op jit(solution)/shard_map/reduce_scatter | solution.py:95
  1570.2 34.5 %reduce-scatter.22.cloned.1.call-done = bf16[512,256]{1,0:T(8,128)(2,1)} async-done(((bf16[512,2048]{1,0:T(8,128)(2,1)}), bf16[512,256]{1,0:T(8,128)(2,1)}) %reduce-scatter.22.cloned.1.call-update) | async-done | bytes 262160 | tf_op jit(solution)/shard_map/reduce_scatter | solution.py:95
  1606.4 52.2 %reduce-scatter.18.cloned.1.call-done = bf16[256,2048]{1,0:T(8,128)(2,1)} async-done(((bf16[1024,2048]{1,0:T(8,128)(2,1)}), bf16[256,2048]{1,0:T(8,128)(2,1)}) %reduce-scatter.18.cloned.1.call-update) | async-done | bytes 1048592 | tf_op jit(solution)/shard_map/reduce_scatter | solution.py:41
  1660.6 41.5 %all-reduce.2 = (f32[2048]{0:T(1024)}, f32[2048]{0:T(1024)}, f32[2048]{0:T(1024)}) all-reduce(f32[2048]{0:T(1024)S(1)} %get-tuple-element.345, f32[2048]{0:T(1024)S(1)} %copy-done.63, f32[2048]{0:T(1024)S(1)} %bitcast.203), channel_id=1, replica_groups=mesh['dp'=8,'tensor'=4] {'dp','tensor'}, use_global_device_ids=true, to_apply=%region_30.31 | all-reduce | flops 6144 | bytes 49152 | tf_op jit(solution)/shard_map/psum | solution.py:359
  1702.1 79.3 %reduce-scatter.24.cloned.1.call-done = bf16[256,2816]{1,0:T(8,128)(2,1)} async-done(((bf16[2048,2816]{1,0:T(8,128)(2,1)}), bf16[256,2816]{1,0:T(8,128)(2,1)}) %reduce-scatter.24.cloned.1.call-update) | async-done | bytes 1441808 | tf_op jit(solution)/shard_map/reduce_scatter | solution.py:83
  1789.2 62.6 %reduce-scatter.20.cloned.1.call-done = bf16[256,1536]{1,0:T(8,128)(2,1)} async-done(((bf16[2048,1536]{1,0:T(8,128)(2,1)}), bf16[256,1536]{1,0:T(8,128)(2,1)}) %reduce-scatter.20.cloned.1.call-update) | async-done | bytes 786448 | tf_op jit(solution)/shard_map/reduce_scatter | solution.py:83
  1854.2 121.7 %all-reduce.5.cloned.1.call-done = f32[2048,8]{0,1:T(8,128)} async-done(((f32[2048,8]{0,1:T(8,128)}), f32[2048,8]{0,1:T(8,128)}) %all-reduce.5.cloned.1.call-update) | async-done | bytes 65552 | tf_op jit(solution)/shard_map/psum | solution.py:359
  (424 shorter events, 543.1 us)
Async XLA Ops:
  13.6 166.7 %all-gather.16.cloned.1.call-start = ((), (), s32[]{:S(2)}) async-start(), calls=%async_computation.17 | async-start | bytes 2359296 | tf_op jit(solution)/shard_map/all_gather | solution.py:60
  14.3 224.8 %reduce-scatter.12.cloned.1.call-start = ((), (), s32[]{:S(2)}) async-start(), calls=%async_computation.18 | async-start | bytes 5242880 | tf_op jit(solution)/shard_map/reduce_scatter | solution.py:41
  187.7 299.7 %all-gather.26.cloned.1.call-start = ((), (), s32[]{:S(2)}) async-start(), calls=%async_computation.23 | async-start | bytes 12976128 | tf_op jit(solution)/shard_map/all_gather | solution.py:53
  190.2 317.8 %all-gather.24.cloned.1.call-start = ((), (), s32[]{:S(2)}) async-start(), calls=%async_computation.22 | async-start | bytes 5242880 | tf_op jit(solution)/shard_map/all_gather | solution.py:37
  244.0 405.4 %all-gather.28.cloned.1.call-start = ((), (), s32[]{:S(2)}) async-start(), calls=%async_computation.24 | async-start | bytes 6488064 | tf_op jit(solution)/shard_map/all_gather | solution.py:60
  244.8 470.3 %all-gather.20.cloned.1.call-start = ((), (), s32[]{:S(2)}) async-start(), calls=%async_computation.20 | async-start | bytes 7208960 | tf_op jit(solution)/shard_map/all_gather | solution.py:247
  261.2 221.0 %all-to-all-start = ((bf16[8,192,2048]{2,1,0:T(8,128)(2,1)}), bf16[8,192,2048]{2,1,0:T(8,128)(2,1)}, u32[]{:S(2)}, u32[]{:S(2)}) async-start(bf16[8,192,2048]{2,1,0:T(8,128)(2,1)} %bitcast.189), calls=%async_computation.1 | async-start | bytes 12582912 | tf_op jit(solution)/shard_map/all_to_all | solution.py:47
  266.1 516.5 %all-gather.18.cloned.1.call-start = ((), (), s32[]{:S(2)}) async-start(), calls=%async_computation.19 | async-start | bytes 7208960 | tf_op jit(solution)/shard_map/all_gather | solution.py:246
  266.8 583.0 %all-gather.22.cloned.1.call-start = ((), (), s32[]{:S(2)}) async-start(), calls=%async_computation.21 | async-start | bytes 7208960 | tf_op jit(solution)/shard_map/all_gather | solution.py:248
  482.1 367.7 %all-to-all-start.2 = ((bf16[8,192,2048]{2,1,0:T(8,128)(2,1)}), bf16[8,192,2048]{2,1,0:T(8,128)(2,1)}, u32[]{:S(2)}, u32[]{:S(2)}) async-start(bf16[8,192,2048]{2,1,0:T(8,128)(2,1)} %bitcast.190), calls=%async_computation.5 | async-start | bytes 12582912 | tf_op jit(solution)/shard_map/all_to_all | solution.py:47
  487.3 424.7 %reduce-scatter.14.cloned.1.call-start = ((), (), s32[]{:S(2)}) async-start(), calls=%async_computation.25 | async-start | bytes 5242880 | tf_op jit(solution)/shard_map/reduce_scatter | solution.py:41
  905.9 143.9 %all-to-all-start.3 = ((bf16[8,192,2048]{2,1,0:T(8,128)(2,1)}), bf16[8,192,2048]{2,1,0:T(8,128)(2,1)}, u32[]{:S(2)}, u32[]{:S(2)}) async-start(bf16[8,192,2048]{2,1,0:T(8,128)(2,1)} %bitcast.193), calls=%async_computation.6 | async-start | bytes 12582912 | tf_op jit(solution)/shard_map/all_to_all | solution.py:47
  910.8 143.8 %all-gather.30.cloned.1.call-start = ((), (), s32[]{:S(2)}) async-start(), calls=%async_computation.26 | async-start | bytes 5242880 | tf_op jit(solution)/shard_map/all_gather | solution.py:37
  1054.5 181.5 %reduce-scatter.16.cloned.1.call-start = ((), (), s32[]{:S(2)}) async-start(), calls=%async_computation.27 | async-start | bytes 5242880 | tf_op jit(solution)/shard_map/reduce_scatter | solution.py:41
  1087.8 214.6 %all-gather.32.cloned.1.call-start = ((), (), s32[]{:S(2)}) async-start(), calls=%async_computation.28 | async-start | bytes 5242880 | tf_op jit(solution)/shard_map/all_gather | solution.py:37
  1244.5 192.2 %reduce-scatter.32.cloned.1.call-start = ((), (), s32[]{:S(2)}) async-start(), calls=%async_computation.37 | async-start | bytes 7208960 | tf_op jit(solution)/shard_map/reduce_scatter | solution.py:332
  1259.0 181.1 %reduce-scatter.30.cloned.1.call-start = ((), (), s32[]{:S(2)}) async-start(), calls=%async_computation.36 | async-start | bytes 7208960 | tf_op jit(solution)/shard_map/reduce_scatter | solution.py:329
  1274.3 226.6 %reduce-scatter.28.cloned.1.call-start = ((), (), s32[]{:S(2)}) async-start(), calls=%async_computation.35 | async-start | bytes 7208960 | tf_op jit(solution)/shard_map/reduce_scatter | solution.py:326
  1289.8 278.0 %reduce-scatter.26.cloned.1.call-start = ((), (), s32[]{:S(2)}) async-start(), calls=%async_computation.34 | async-start | bytes 6488064 | tf_op jit(solution)/shard_map/reduce_scatter | solution.py:95
  1302.3 302.4 %reduce-scatter.22.cloned.1.call-start = ((), (), s32[]{:S(2)}) async-start(), calls=%async_computation.31 | async-start | bytes 2359296 | tf_op jit(solution)/shard_map/reduce_scatter | solution.py:95
  1310.3 348.4 %reduce-scatter.18.cloned.1.call-start = ((), (), s32[]{:S(2)}) async-start(), calls=%async_computation.29 | async-start | bytes 5242880 | tf_op jit(solution)/shard_map/reduce_scatter | solution.py:41
  1387.9 393.4 %reduce-scatter.24.cloned.1.call-start = ((), (), s32[]{:S(2)}) async-start(), calls=%async_computation.33 | async-start | bytes 12976128 | tf_op jit(solution)/shard_map/reduce_scatter | solution.py:83
  1406.5 445.4 %reduce-scatter.20.cloned.1.call-start = ((), (), s32[]{:S(2)}) async-start(), calls=%async_computation.30 | async-start | bytes 7077888 | tf_op jit(solution)/shard_map/reduce_scatter | solution.py:83
  1419.8 556.1 %all-reduce.5.cloned.1.call-start = ((), (), s32[]{:S(2)}) async-start(), calls=%async_computation.32 | async-start | bytes 131072 | tf_op jit(solution)/shard_map/psum | solution.py:359
  (107 other events, 4293.3 us)
Sparse Core Ops, SparseCore 0:
  12.7 55.2 all-gather.11
  70.2 64.6 all-gather.13
  136.5 29.2 all-gather.15
  187.8 51.2 reduce-scatter.11
  241.2 213.6 all-gather.25
  456.6 51.3 all-gather.23
  509.6 139.7 all-gather.27
  651.2 63.7 all-gather.19
  716.9 65.6 all-gather.17
  784.3 65.5 all-gather.21
  852.8 52.5 reduce-scatter.13
  915.0 52.9 all-gather.29
  1087.9 52.9 reduce-scatter.15
  1244.7 50.4 all-gather.31
  1298.0 65.6 reduce-scatter.31
  1366.6 65.6 reduce-scatter.29
  1435.1 65.6 reduce-scatter.27
  1503.0 64.7 reduce-scatter.25
  1570.1 34.5 reduce-scatter.21
  1607.5 51.1 reduce-scatter.17
  1661.0 120.2 reduce-scatter.23
  1783.6 68.1 reduce-scatter.19
  1858.0 117.7 all-reduce.4
where the time goes:
time: 2000 us; the launch traced here: 1980 us
  waiting for transfers between devices  1320 us (66%)
  matrix products  337 us (17%)
  local copies, waits for them, and re-layouts  129 us (6%)
  other arithmetic  97.4 us (5%)
  blocking collectives  55 us (3%)
  starting transfers between devices  21.4 us (1%)
    all_to_all x4, waiting for transfers between devices, trade_slots(): lax.all_to_all(slot_rows, 'dp', split_axis=0, concat_axis=0, tiled=True)  378 us
    reduce_scatter x2, waiting for transfers between devices, grads_in(): lax.psum_scatter(lax.dot_general(gathered, grad_cols, CONTRACT_FIRST, pre...  142 us
    psum x1, waiting for transfers between devices, local(): lax.psum((d_attn_gain_part, d_moe_gain_part, d_router_part, d_sigmoid_par...  122 us
    all_gather x2, waiting for transfers between devices, project_out(): lax.all_gather(weight, 'dp', axis=1, tiled=True)  118 us
    reduce_scatter x4, waiting for transfers between devices, split_rows(): lax.psum_scatter(partial_sum.astype(jnp.bfloat16), 'tensor', scatter_dime...  101 us
    reduce_scatter x2, waiting for transfers between devices, grads_out(): lax.psum_scatter(product.astype(jnp.bfloat16), 'dp', scatter_dimension=1,...  98.3 us
    all_gather x4, waiting for transfers between devices, group_rows(): return lax.all_gather(local_rows, 'tensor', axis=0, tiled=True)  74.2 us
    all_gather x2, waiting for transfers between devices, project_in(): lax.all_gather(weight, 'dp', axis=0, tiled=True)  67 us
  transfers between devices with their start and end apart: 27, of which 18 were waited for; matrix products, arithmetic and copies ran while one was open for 26% of the time, Pallas kernels for 0%

commit v1 on v0

v1 whole, which is shorter than its diff:
```python
import jax
import jax.numpy as jnp
from jax import lax
from jax.sharding import PartitionSpec as P

DH = 128


EPS = 1e-06
CLIP_LIMIT = 6.0
NEG = -1e30
HIGH = lax.Precision.HIGHEST
CONTRACT_LAST = (((1,), (1,)), ((), ()))
CONTRACT_FIRST = (((0,), (0,)), ((), ()))


def norm_rows(inputs, gain):
    factor = lax.rsqrt(jnp.mean(inputs * inputs, axis=-1, keepdims=True) + EPS)
    return (inputs * factor * gain, factor)


def norm_back(inputs, factor, gain, upstream):
    scaled = upstream * gain
    inner = jnp.mean(scaled * inputs, axis=-1, keepdims=True)
    return (
        factor * scaled - inputs * (factor * factor * factor) * inner,
        jnp.sum(upstream * inputs * factor, axis=0),
    )


def pairs(count, bit):
    return [(index, index ^ bit) for index in range(count)]


def swap(values_in, bit, axis_name="tensor"):
    return lax.ppermute(values_in, axis_name, pairs(lax.axis_size(axis_name), bit))


def halves(values_in, axis):
    middle_at = values_in.shape[axis] // 2
    return (
        lax.slice_in_dim(values_in, 0, middle_at, axis=axis),
        lax.slice_in_dim(values_in, middle_at, values_in.shape[axis], axis=axis),
    )


def relay_gather(block):
    across = swap(block, 1)
    along = swap(block, 2)
    cut = 1 if block.ndim > 2 else 0
    first, _ = halves(along, cut)
    _, second = halves(across, cut)
    diagonal = jnp.concatenate([swap(first, 1), swap(second, 2)], axis=cut)
    here = lax.axis_index("tensor")
    odd, high = (here & 1) == 1, (here & 2) == 2
    low_even, low_odd = jnp.where(odd, across, block), jnp.where(odd, block, across)
    high_even, high_odd = jnp.where(odd, diagonal, along), jnp.where(odd, along, diagonal)
    return (
        jnp.where(high, high_even, low_even),
        jnp.where(high, high_odd, low_odd),
        jnp.where(high, low_even, high_even),
        jnp.where(high, low_odd, high_odd),
    )


def group_gather(block, axis):
    if lax.axis_size("tensor") != 4:
        return lax.all_gather(block, "tensor", axis=axis, tiled=True)
    return jnp.concatenate(relay_gather(block), axis=axis)


def group_scatter(partial, axis):
    count = lax.axis_size("tensor")
    if count != 4:
        return lax.psum_scatter(
            partial, "tensor", scatter_dimension=axis, tiled=True
        ).astype(jnp.float32)
    here = lax.axis_index("tensor")
    size = partial.shape[axis] // count

    def block(other):
        return lax.dynamic_slice_in_dim(partial, (here ^ other) * size, size, axis)

    cut = 1 if partial.ndim > 2 else 0
    far = halves(block(3), cut)
    over_x, over_y = swap(far[0], 1), swap(far[1], 2)
    near_y, near_x = halves(block(2), cut), halves(block(1), cut)
    wide = jnp.float32
    send_y = jnp.concatenate(
        [(near_y[0].astype(wide) + over_x.astype(wide)).astype(partial.dtype), near_y[1]], axis=cut
    )
    send_x = jnp.concatenate(
        [near_x[0], (near_x[1].astype(wide) + over_y.astype(wide)).astype(partial.dtype)], axis=cut
    )
    from_y, from_x = swap(send_y, 2), swap(send_x, 1)
    return block(0).astype(wide) + from_y.astype(wide) + from_x.astype(wide)


def column_gather(rows):
    return lax.all_gather(rows, "dp", axis=0, tiled=True)


def column_scatter(partial, axis):
    return lax.psum_scatter(
        partial.astype(jnp.bfloat16), "dp", scatter_dimension=axis, tiled=True
    ).astype(jnp.float32)


def trade(blocks, axis_name):
    return lax.all_to_all(blocks, axis_name, split_axis=0, concat_axis=0, tiled=True)


def butterfly(values_in, combine, axis_names):
    for axis_name in axis_names:
        bit = 1
        while bit < lax.axis_size(axis_name):
            values_in = combine(values_in, swap(values_in, bit, axis_name))
            bit *= 2
    return values_in


def times(left, right):
    return jnp.dot(left, right, preferred_element_type=jnp.float32)


def times_last(left, right):
    return lax.dot_general(left, right, CONTRACT_LAST, preferred_element_type=jnp.float32)


def times_first(left, right):
    return lax.dot_general(left, right, CONTRACT_FIRST, preferred_element_type=jnp.float32)


def slice_width(hidden_width, share):
    return -(-hidden_width // (128 * share)) * 128


def spread_in(weights):
    count, owners = lax.axis_size("tensor"), lax.axis_size("dp")
    share = owners // count
    rows, hidden_width = weights[0].shape
    width = slice_width(hidden_width, share)
    piece = rows // count
    padded = jnp.stack(
        [jnp.pad(w, ((0, 0), (0, share * width - hidden_width))) for w in weights], axis=0
    )
    blocks = padded.reshape(2, count, piece, share * width).transpose(1, 0, 2, 3)
    blocks = trade(blocks, "tensor").reshape(count, 2, piece, share, width)
    blocks = blocks.transpose(0, 3, 1, 2, 4).reshape(owners, 2, piece, width)
    blocks = trade(blocks, "dp")
    whole = group_gather(blocks.reshape(1, owners, 2, piece, width), 0)
    whole = whole.transpose(2, 1, 0, 3, 4).reshape(2, owners * rows, width)
    return whole[0], whole[1]


def spread_in_back(grads, rows, hidden_width):
    count, owners = lax.axis_size("tensor"), lax.axis_size("dp")
    share = owners // count
    width = grads[0].shape[1]
    piece = rows // count
    stacked = jnp.stack(grads, axis=0).reshape(2, owners, count, piece, width)
    stacked = stacked.transpose(2, 1, 0, 3, 4)
    blocks = group_scatter(stacked, 0).astype(jnp.bfloat16).reshape(owners, 2, piece, width)
    blocks = trade(blocks, "dp").reshape(count, share, 2, piece, width)
    blocks = blocks.transpose(0, 2, 3, 1, 4).reshape(count, 2, piece, share * width)
    blocks = trade(blocks, "tensor").transpose(1, 0, 2, 3).reshape(2, rows, share * width)
    blocks = blocks[:, :, :hidden_width].astype(jnp.float32)
    return blocks[0], blocks[1]


def spread_out(weight):
    count, owners = lax.axis_size("tensor"), lax.axis_size("dp")
    share = owners // count
    hidden_width, columns = weight.shape
    width = slice_width(hidden_width, share)
    padded = jnp.pad(weight, ((0, share * width - hidden_width), (0, 0)))
    blocks = padded.reshape(share, count, width // count, columns).transpose(1, 0, 2, 3)
    blocks = trade(blocks, "tensor").reshape(owners, width // count, columns)
    blocks = trade(blocks, "dp").transpose(1, 0, 2).reshape(width // count, owners * columns)
    return group_gather(blocks, 0)


def spread_out_back(grad, hidden_width, columns):
    count, owners = lax.axis_size("tensor"), lax.axis_size("dp")
    share = owners // count
    width = grad.shape[0]
    piece = width // count
    blocks = group_scatter(grad, 0).astype(jnp.bfloat16).reshape(piece, owners, columns)
    blocks = trade(blocks.transpose(1, 0, 2), "dp").reshape(count, share, piece, columns)
    blocks = trade(blocks, "tensor").transpose(1, 0, 2, 3).reshape(share * width, columns)
    return blocks[:hidden_width].astype(jnp.float32)


def attention_forward(queries, keys_in, values_in, length, factor):
    seq_len = queries.shape[0]
    block_len = min(512, seq_len)
    position = jnp.arange(seq_len, dtype=jnp.int32)

    def one_block(offset):
        rows_here = offset + jnp.arange(block_len, dtype=jnp.int32)
        query_block = lax.dynamic_slice_in_dim(queries, offset, block_len, 0)
        allowed = (position[None, :] <= rows_here[:, None]) & (position[None, :] < length)
        raw_scores = (
            jnp.einsum("qhd,khd->hqk", query_block, keys_in, preferred_element_type=jnp.float32)
            * factor
        )
        scores = jnp.where(allowed[None], raw_scores, NEG)
        highest = jnp.max(scores, axis=2, keepdims=True)
        log_total = highest + jnp.log(jnp.sum(jnp.exp(scores - highest), axis=2, keepdims=True))
        weights = jnp.exp(scores - log_total).astype(jnp.bfloat16)
        attended = jnp.einsum(
            "hqk,khd->qhd", weights, values_in, preferred_element_type=jnp.float32
        )
        counted = allowed & (rows_here[:, None] < length)
        peak_here = jnp.max(jnp.where(counted[None], raw_scores, NEG), axis=(1, 2))
        return (attended.astype(jnp.bfloat16), log_total[:, :, 0], peak_here)

    offsets = jnp.arange(seq_len // block_len, dtype=jnp.int32) * block_len
    attended, log_totals, peaks = lax.map(one_block, offsets)
    return (attended.reshape(seq_len, -1), log_totals, jnp.max(peaks, axis=0))


def attention_backward(queries, keys_in, values_in, grad_out, log_totals, length, factor):
    seq_len = queries.shape[0]
    block_len = log_totals.shape[2]
    position = jnp.arange(seq_len, dtype=jnp.int32)

    def one_block(sums, packed):
        key_sum, value_sum = sums
        offset, log_total = packed
        rows_here = offset + jnp.arange(block_len, dtype=jnp.int32)
        query_block = lax.dynamic_slice_in_dim(queries, offset, block_len, 0)
        grad_block = lax.dynamic_slice_in_dim(grad_out, offset, block_len, 0)
        allowed = (position[None, :] <= rows_here[:, None]) & (position[None, :] < length)
        raw_scores = (
            jnp.einsum("qhd,khd->hqk", query_block, keys_in, preferred_element_type=jnp.float32)
            * factor
        )
        scores = jnp.where(allowed[None], raw_scores, NEG)
        probs = jnp.exp(scores - log_total[:, :, None])
        weights = probs.astype(jnp.bfloat16)
        along = jnp.einsum(
            "qhd,khd->hqk", grad_block, values_in, preferred_element_type=jnp.float32
        )
        inner = jnp.sum(probs * along, axis=2, keepdims=True)
        grad_scores = (probs * (along - inner)).astype(jnp.bfloat16)
        grad_query = (
            jnp.einsum("hqk,khd->qhd", grad_scores, keys_in, preferred_element_type=jnp.float32)
            * factor
        )
        key_sum = (
            key_sum
            + jnp.einsum(
                "hqk,qhd->khd", grad_scores, query_block, preferred_element_type=jnp.float32
            )
            * factor
        )
        value_sum = value_sum + jnp.einsum(
            "hqk,qhd->khd", weights, grad_block, preferred_element_type=jnp.float32
        )
        return ((key_sum, value_sum), grad_query.astype(jnp.bfloat16))

    offsets = jnp.arange(seq_len // block_len, dtype=jnp.int32) * block_len
    start_zero = jnp.zeros(keys_in.shape, jnp.float32)
    (key_sum, value_sum), grad_query = lax.scan(
        one_block, (start_zero, start_zero), (offsets, log_totals)
    )
    return (
        grad_query.reshape(seq_len, -1),
        key_sum.astype(jnp.bfloat16).reshape(seq_len, -1),
        value_sum.astype(jnp.bfloat16).reshape(seq_len, -1),
    )


def local(
    tokens,
    lengths,
    routes,
    attn_gain,
    w_query,
    w_key,
    w_value,
    w_output,
    moe_gain,
    w_router,
    w_sigmoid,
    shared_gate,
    shared_up,
    shared_down,
    expert_gate,
    expert_up,
    expert_down,
    cotangent,
):
    low = jnp.bfloat16
    factor = DH ** (-0.5)
    inputs = tokens.astype(jnp.float32)
    normed, inv_one = norm_rows(inputs, attn_gain)
    gathered_one = group_gather(normed.astype(low), 0)
    seq_len = gathered_one.shape[0]
    width = w_query.shape[1]
    in_weights = column_gather(jnp.concatenate([w_query, w_key, w_value], axis=1))
    out_weight = lax.all_gather(w_output, "dp", axis=1, tiled=True)
    projected = times(gathered_one, in_weights).astype(low)
    queries = projected[:, :width].reshape(seq_len, -1, DH)
    keys_in = projected[:, width : 2 * width].reshape(seq_len, -1, DH)
    values_in = projected[:, 2 * width :].reshape(seq_len, -1, DH)
    length = lengths[0]
    attended, log_totals, peaks = attention_forward(queries, keys_in, values_in, length, factor)
    peaks = butterfly(peaks, jnp.maximum, ("dp",))
    middle = inputs + group_scatter(times(attended, out_weight).astype(low), 0)
    moe_norm, inv_two = norm_rows(middle, moe_gain)
    moe_low = moe_norm.astype(low)
    moe_wide = moe_low.astype(jnp.float32)
    experts = w_router.shape[1]
    owners = lax.axis_size("dp")
    rows_dev, route_count = routes.shape
    column_rows = owners * rows_dev
    logits = jnp.dot(moe_wide, w_router, precision=HIGH)
    picked = (routes[:, :, None] == jnp.arange(experts, dtype=jnp.int32)[None, None, :]).astype(
        jnp.float32
    )
    chosen = jnp.sum(picked * logits[:, None, :], axis=2)
    gates = jax.nn.softmax(chosen, axis=1)
    mixing = jax.nn.sigmoid(jnp.dot(moe_wide, w_sigmoid, precision=HIGH))
    gate_of = jnp.sum(picked * gates[:, :, None], axis=1)
    scales = jnp.stack([gate_of.T, jnp.broadcast_to(mixing[None], (experts, rows_dev))], axis=1)
    scales = trade(scales, "dp")
    scale_routed = scales[:, 0].reshape(column_rows, 1)
    scale_shared = scales[:, 1].reshape(column_rows, 1)
    column = column_gather(moe_low)
    upstream_column = column_gather(cotangent)
    full_gate = group_gather(expert_gate[0], 0)
    full_up = group_gather(expert_up[0], 0)
    full_down = group_gather(expert_down[0], 1)
    part_gate, part_up = spread_in((shared_gate, shared_up))
    part_down = spread_out(shared_down)

    def branch(gate_weight, up_weight, down_weight, scale):
        gate_pre = times(column, gate_weight)
        up_pre = times(column, up_weight)
        raw = times_last(upstream_column, down_weight)
        sigma = jax.nn.sigmoid(gate_pre)
        activated = gate_pre * sigma
        hidden = activated * up_pre
        inner = jnp.sum(hidden * raw, axis=1)
        scaled = raw * scale
        d_gate = (scaled * up_pre * (sigma * (1.0 + gate_pre * (1.0 - sigma)))).astype(low)
        d_up = (scaled * activated).astype(low)
        hidden = (hidden * scale).astype(low)
        d_rows = times_last(d_gate, gate_weight) + times_last(d_up, up_weight)
        return (hidden, inner, d_gate, d_up, d_rows)

    hidden_e, inner_e, d_gate_e, d_up_e, d_rows_e = branch(
        full_gate, full_up, full_down, scale_routed
    )
    hidden_s, inner_s, d_gate_s, d_up_s, d_rows_s = branch(
        part_gate, part_up, part_down, scale_shared
    )
    d_moe = column_scatter((d_rows_e + d_rows_s).astype(low), 0)
    inner = trade(
        jnp.stack([inner_e.reshape(owners, rows_dev), inner_s.reshape(owners, rows_dev)], axis=1),
        "dp",
    )
    combined = middle + column_scatter(
        (times(hidden_e, full_down) + times(hidden_s, part_down)).astype(low), 0
    )
    upstream = cotangent.astype(jnp.float32)
    d_mixing = mixing * (1.0 - mixing) * jnp.sum(inner[:, 1], axis=0)
    d_gates = jnp.sum(picked * inner[:, 0].T[:, None, :], axis=2)
    d_chosen = gates * (d_gates - jnp.sum(gates * d_gates, axis=1, keepdims=True))
    d_logits = jnp.sum(picked * d_chosen[:, :, None], axis=1)
    d_moe = (
        d_moe
        + jnp.dot(d_logits, w_router.T, precision=HIGH)
        + d_mixing[:, None] * w_sigmoid[None, :]
    )
    d_router_part = jnp.dot(d_logits.T, moe_wide, precision=HIGH)
    d_sigmoid_part = jnp.dot(d_mixing, moe_wide, precision=HIGH)
    d_middle_norm, d_moe_gain_part = norm_back(middle, inv_two, moe_gain, d_moe)
    d_middle = upstream + d_middle_norm
    small_sums = butterfly(
        jnp.concatenate([d_router_part, d_sigmoid_part[None], d_moe_gain_part[None]], axis=0),
        jnp.add,
        ("tensor", "dp"),
    )
    d_expert_gate = group_scatter(times_first(column, d_gate_e).astype(low), 0)
    d_expert_up = group_scatter(times_first(column, d_up_e).astype(low), 0)
    d_expert_down = group_scatter(times_first(hidden_e, upstream_column).astype(low), 1)
    d_shared_gate, d_shared_up = spread_in_back(
        (times_first(column, d_gate_s).astype(low), times_first(column, d_up_s).astype(low)),
        *shared_gate.shape,
    )
    d_shared_down = spread_out_back(
        times_first(hidden_s, upstream_column).astype(low), *shared_down.shape
    )
    whole_middle = group_gather(d_middle.astype(low), 0)
    d_w_output = column_scatter(times_first(attended, whole_middle), 1)
    d_attended = times_last(whole_middle, out_weight).astype(low).reshape(seq_len, -1, DH)
    d_queries, d_keys, d_values = attention_backward(
        queries, keys_in, values_in, d_attended, log_totals, length, factor
    )
    d_projected = jnp.concatenate([d_queries, d_keys, d_values], axis=1)
    d_in_weights = column_scatter(times_first(gathered_one, d_projected), 0)
    d_normed = group_scatter(times_last(d_projected, in_weights).astype(low), 0)
    d_inputs_norm, d_attn_gain_part = norm_back(inputs, inv_one, attn_gain, d_normed)
    d_tokens = d_middle + d_inputs_norm
    d_attn_gain = butterfly(d_attn_gain_part.reshape(-1, 128), jnp.add, ("tensor", "dp")).reshape(-1)
    clip_scale = jnp.sqrt(CLIP_LIMIT / jnp.maximum(peaks, CLIP_LIMIT))
    columns = jnp.repeat(clip_scale, DH)
    query_clipped = (w_query.astype(jnp.float32) * columns[None, :]).astype(low)
    key_clipped = (w_key.astype(jnp.float32) * columns[None, :]).astype(low)
    return (
        combined.astype(low),
        d_tokens,
        d_attn_gain,
        d_in_weights[:, :width],
        d_in_weights[:, width : 2 * width],
        d_in_weights[:, 2 * width :],
        d_w_output,
        small_sums[experts + 1],
        small_sums[:experts].T,
        small_sums[experts],
        d_shared_gate,
        d_shared_up,
        d_shared_down,
        d_expert_gate[None],
        d_expert_up[None],
        d_expert_down[None],
        clip_scale,
        query_clipped,
        key_clipped,
    )


def solution(mesh):
    placed = (
        P(("dp", "tensor"), None),
        P("dp"),
        P(("dp", "tensor"), None),
        P(),
        P("dp", "tensor"),
        P("dp", "tensor"),
        P("dp", "tensor"),
        P("tensor", "dp"),
        P(),
        P(),
        P(),
        P("dp", "tensor"),
        P("dp", "tensor"),
        P("tensor", "dp"),
        P("dp", "tensor", None),
        P("dp", "tensor", None),
        P("dp", None, "tensor"),
        P(("dp", "tensor"), None),
    )
    return jax.shard_map(
        local,
        mesh=mesh,
        in_specs=placed,
        out_specs=(
            P(("dp", "tensor"), None),
            P(("dp", "tensor"), None),
            P(),
            P("dp", "tensor"),
            P("dp", "tensor"),
            P("dp", "tensor"),
            P("tensor", "dp"),
            P(),
            P(),
            P(),
            P("dp", "tensor"),
            P("dp", "tensor"),
            P("tensor", "dp"),
            P("dp", "tensor", None),
            P("dp", "tensor", None),
            P("dp", None, "tensor"),
            P("tensor"),
            P("dp", "tensor"),
            P("dp", "tensor"),
        ),
        check_vma=False,
    )
```

time: 2000 us -> 1280 us (0.64)
  waiting for transfers between devices: 1320 us -> 494 us
  starting transfers between devices: 21.4 us -> 122 us
  other arithmetic: 97.4 us -> 163 us
  local copies, waits for them, and re-layouts: 129 us -> 78.2 us
  blocking collectives: 55 us -> 8.48 us
  matrix products: 337 us -> 378 us
    all_gather x11 -> x4, waiting for transfers between devices: 419 us -> 19.5 us  [the longest x3 19.5 us: column_gather(): return lax.all_gather(rows, 'dp', axis=0, tiled=True)]
    ppermute x0 -> x69, waiting for transfers between devices: none -> 389 us  [swap(): lax.ppermute(values_in, axis_name, pairs(lax.axis_size(axis_name), bit))]
    reduce_scatter x11 -> x4, waiting for transfers between devices: 399 us -> 13.8 us  [column_scatter(): lax.psum_scatter(partial.astype(jnp.bfloat16), 'dp', scatter_dimension=ax...]
    all_to_all x4 -> x9, waiting for transfers between devices: 378 us -> 70.8 us  [trade(): lax.all_to_all(blocks, axis_name, split_axis=0, concat_axis=0, tiled=True)]
    psum x1 -> x0, waiting for transfers between devices: 122 us -> none  [local(): lax.psum((d_attn_gain_part, d_moe_gain_part, d_router_part, d_sigmoid_par...]
    ppermute x0 -> x69, starting transfers between devices: none -> 82.4 us  [swap(): lax.ppermute(values_in, axis_name, pairs(lax.axis_size(axis_name), bit))]
    gather x4 -> x0, local copies, waits for them, and re-layouts: 47.3 us -> none  [the longest x1 15.4 us: local(): padded_grad[slot_owner].reshape(experts, capacity, model_width)]
    psum x1 -> x0, blocking collectives: 41.5 us -> none  [local(): lax.psum((d_attn_gain_part, d_moe_gain_part, d_router_part, d_sigmoid_par...]
  transfers between devices with their start and end apart: 27 -> 86, of which waited for: 18 -> 45; matrix products, arithmetic and copies ran while one was open for 26% -> 34% of each run, Pallas kernels for 0% -> 0%
where the time goes in v1:
time: 1280 us; the launch traced here: 1270 us
  waiting for transfers between devices  494 us (39%)
  matrix products  378 us (30%)
  other arithmetic  163 us (13%)
  starting transfers between devices  122 us (10%)
  local copies, waits for them, and re-layouts  78.2 us (6%)
  between operations  16.4 us (1%)
    ppermute x69, waiting for transfers between devices, swap(): lax.ppermute(values_in, axis_name, pairs(lax.axis_size(axis_name), bit))  389 us
    dot_general x8, matrix products, times_last(): lax.dot_general(left, right, CONTRACT_LAST, preferred_element_type=jnp.fl...  123 us
    dot_general x8, matrix products, times(): return jnp.dot(left, right, preferred_element_type=jnp.float32)  111 us
    dot_general x8, matrix products, times_first(): lax.dot_general(left, right, CONTRACT_FIRST, preferred_element_type=jnp.f...  92 us
    ppermute x69, starting transfers between devices, swap(): lax.ppermute(values_in, axis_name, pairs(lax.axis_size(axis_name), bit))  82.4 us
    all_to_all x9, waiting for transfers between devices, trade(): lax.all_to_all(blocks, axis_name, split_axis=0, concat_axis=0, tiled=True)  70.8 us
    all_to_all x9, starting transfers between devices, trade(): lax.all_to_all(blocks, axis_name, split_axis=0, concat_axis=0, tiled=True)  39.1 us
  transfers between devices with their start and end apart: 86, of which 45 were waited for; matrix products, arithmetic and copies ran while one was open for 34% of the time, Pallas kernels for 0%

profile of v1, /device:TPU:0, one launch (start us, length us, event | category | flops | bytes accessed | tf_op | source)
XLA Modules:
  0.0 1267.6 jit_solution(7134105557843675101)
XLA Ops:
  16.4 21.7 %collective-permute-done = bf16[256,2048]{1,0:T(8,128)(2,1)S(1)} collective-permute-done((bf16[256,2048]{1,0:T(8,128)(2,1)S(1)}, bf16[256,2048]{1,0:T(8,128)(2,1)S(1)}, u32[]{:S(2)}, u32[]{:S(2)}) %collective-permute-start) | collective-permute-done | bytes 1048608 | tf_op jit(solution)/shard_map/ppermute | solution.py:36
  58.2 19.5 %all-gather.5.cloned.1.call-done = bf16[2048,1536]{1,0:T(8,128)(2,1)} async-done(((bf16[256,1536]{1,0:T(8,128)(2,1)}), bf16[2048,1536]{1,0:T(8,128)(2,1)}) %all-gather.5.cloned.1.call-update) | async-done | bytes 6291472 | tf_op jit(solution)/shard_map/all_gather | solution.py:100
  91.3 32.9 %while.32 = (s32[]{:T(128)}, bf16[2,512,4,128]{3,2,1,0:T(4,128)(2,1)}, f32[2,4,512]{2,1,0:T(4,128)S(1)}, f32[2,4]{1,0:T(2,128)S(1)}, s32[2]{0:T(128)S(1)}, /*ind...) while((s32[]{:T(128)}, ...), condition=%wide.region_5.6_spmd.clone.clone, body=%wide.region_1.5_spmd.clone.clone.sunk | while | flops 1102840320 | bytes 40967468 | solution.py:219
  152.7 21.2 %collective-permute-done.5 = bf16[256,2048]{1,0:T(8,128)(2,1)} collective-permute-done((bf16[256,2048]{1,0:T(8,128)(2,1)S(1)}, bf16[256,2048]{1,0:T(8,128)(2,1)}, u32[]{:S(2)}, u32[]{:S(2)}) %collective-permute-start.5) | collective-permute-done | bytes 1048608 | tf_op jit(solution)/shard_map/ppermute | solution.py:36
  201.1 17.7 %all-to-all-done.1 = bf16[4,2,64,1536]{3,2,1,0:T(8,128)(2,1)S(1)} async-done(((bf16[4,2,64,1536]{3,2,1,0:T(8,128)(2,1)}), bf16[4,2,64,1536]{3,2,1,0:T(8,128)(2,1)S(1)}, u32[]{:S(2)}, u32[]{:S(2)}) %all-to-all-start.1) | async-done | bytes 1572896 | tf_op jit(solution)/shard_map/all_to_all | solution.py:110
  227.5 22.3 %collective-permute-done.12 = bf16[512,1408]{1,0:T(8,128)(2,1)} collective-permute-done((bf16[512,1408]{1,0:T(8,128)(2,1)}, bf16[512,1408]{1,0:T(8,128)(2,1)}, u32[]{:S(2)}, u32[]{:S(2)}) %collective-permute-start.12) | collective-permute-done | bytes 1441824 | tf_op jit(solution)/shard_map/ppermute | solution.py:36
  292.3 19.2 %collective-permute-done.16 = bf16[1408,512]{1,0:T(8,128)(2,1)S(1)} collective-permute-done((bf16[1408,512]{1,0:T(8,128)(2,1)}, bf16[1408,512]{1,0:T(8,128)(2,1)S(1)}, u32[]{:S(2)}, u32[]{:S(2)}) %collective-permute-start.16) | collective-permute-done | bytes 1441824 | tf_op jit(solution)/shard_map/ppermute | solution.py:36
  391.0 34.1 %collective-permute-done.25 = bf16[96,2048]{1,0:T(8,128)(2,1)S(1)} collective-permute-done((bf16[96,2048]{1,0:T(8,128)(2,1)S(1)}, bf16[96,2048]{1,0:T(8,128)(2,1)S(1)}, u32[]{:S(2)}, u32[]{:S(2)}) %collective-permute-start.25) | collective-permute-done | bytes 393248 | tf_op jit(solution)/shard_map/ppermute | solution.py:36
  452.1 19.8 %fusion.64 = f32[2048,1408]{0,1:T(8,128)} fusion(bf16[2048,2048]{1,0:T(8,128)(2,1)} %all-gather.9.cloned.1.call-done, bf16[512,1408]{1,0:T(8,128)(2,1)} %get-tuple-element.486, bf16[512,1408]{1,0:T(8,128)(2,1)} %get-tuple-element.485, bf16[512,1408]{1,0:T(8,128)(2,1)} %get-tuple-element.484, bf16[512,1408]{1,0:T(8,128)(2,1)} %get-tuple-element.483), kind=kOutput, calls=%fused_computation.230 | convolution fusion | flops 11834228736 | bytes 25690112 | tf_op jit(solution)/shard_map/dot_general | solution.py:123
  471.9 18.0 %fusion.65 = f32[2048,1408]{0,1:T(8,128)} fusion(bf16[2048,2048]{1,0:T(8,128)(2,1)} %all-gather.9.cloned.1.call-done, bf16[512,1408]{1,0:T(8,128)(2,1)} %get-tuple-element.482, bf16[512,1408]{1,0:T(8,128)(2,1)S(1)} %copy-done.69, bf16[512,1408]{1,0:T(8,128)(2,1)S(1)} %copy-done.68, bf16[512,1408]{1,0:T(8,128)(2,1)S(1)} %copy-done.66), kind=kOutput, calls=%fused_computation.231 | convolution fusion | flops 11834228736 | bytes 25690112 | tf_op jit(solution)/shard_map/dot_general | solution.py:123
  489.8 22.6 %fusion.39 = (f32[2048]{0:T(1024)S(1)}, f32[1408,2048]{1,0:T(8,128)}) fusion(f32[2048,1408]{0,1:T(8,128)} %fusion.64, f32[2048,1408]{0,1:T(8,128)} %fusion.65, bf16[2048,2048]{1,0:T(8,128)(2,1)} %all-gather.11.cloned.1.call-done, bf16[1408,512]{1,0:T(8,128)(2,1)} %get-tuple-element.490, bf16[1408,512]{1,0:T(8,128)(2,1)} %get-tuple-element.489, ...), kind=kOutput, calls=%fused_computation.61 | convolution fusion | flops 11854411776 | bytes 48766976 | tf_op jit(solution)/shard_map/dot_general | solution.py:127
  570.3 21.0 %multiply_convert_fusion.2 = (bf16[2048,1408]{0,1:T(8,128)(2,1)}, bf16[2048,1408]{0,1:T(8,128)(2,1)}, bf16[2048,1408]{0,1:T(8,128)(2,1)}) fusion(f32[2048,1408]{0,1:T(8,128)} %fusion.65, f32[2048,1408]{0,1:T(8,128)} %fusion.64, f32[1408,2048]{1,0:T(8,128)} %get-tuple-element.549, f32[2048]{0:T(1024)S(1)} %bitcast.301), kind=kLoop, calls=%fused_computation.63 | loop fusion | flops 49020928 | bytes 51912704 | tf_op jit(solution)/shard_map/convert_element_type | solution.py:348
  591.3 21.1 %fusion.63 = f32[2048,2048]{1,0:T(8,128)} fusion(bf16[2048,1408]{0,1:T(8,128)(2,1)} %get-tuple-element.446, bf16[512,1408]{1,0:T(8,128)(2,1)} %get-tuple-element.486, bf16[512,1408]{1,0:T(8,128)(2,1)} %get-tuple-element.485, bf16[512,1408]{1,0:T(8,128)(2,1)} %get-tuple-element.484, bf16[512,1408]{1,0:T(8,128)(2,1)S(1)} %copy-done.65), kind=kOutput, calls=%fused_computation.229 | convolution fusion | flops 11834228736 | bytes 28311552 | tf_op jit(solution)/shard_map/dot_general | solution.py:127
  642.1 27.4 %add_convert_fusion = bf16[2048,2048]{1,0:T(8,128)(2,1)} fusion(f32[2048,2048]{1,0:T(8,128)} %fusion.100, f32[2048,2048]{1,0:T(8,128)} %fusion.101, f32[2048,2048]{1,0:T(8,128)} %fusion.63, bf16[2048,1408]{0,1:T(8,128)(2,1)} %get-tuple-element.445, bf16[512,1408]{1,0:T(8,128)(2,1)} %get-tuple-element.482, bf16[512,1408]{1,0:T(8,128)(2,1)} %get-tuple-element.481, ...), kind=kOutput, calls=%fused_computation.57 | convolution fusion | flops 11851005952 | bytes 70254592 | tf_op jit(solution)/shard_map/dot_general | solution.py:127
  695.7 21.2 %add_convert_fusion.1 = bf16[2048,2048]{1,0:T(8,128)(2,1)} fusion(f32[2048,2048]{1,0:T(8,128)} %fusion.69, bf16[2048,1408]{0,1:T(8,128)(2,1)} %get-tuple-element.447, bf16[1408,512]{1,0:T(8,128)(2,1)} %get-tuple-element.490, bf16[1408,512]{1,0:T(8,128)(2,1)} %get-tuple-element.489, bf16[1408,512]{1,0:T(8,128)(2,1)S(1)} %copy-done.64, ...), kind=kOutput, calls=%fused_computation.58 | convolution fusion | flops 11842617344 | bytes 36700160 | tf_op jit(solution)/shard_map/dot_general | solution.py:123
  717.0 16.5 %convolution_convert_fusion = bf16[1408,2048]{1,0:T(8,128)(2,1)S(1)} fusion(bf16[2048,1408]{0,1:T(8,128)(2,1)} %get-tuple-element.447, bf16[2048,2048]{1,0:T(8,128)(2,1)} %all-gather.11.cloned.1.call-done), kind=kOutput, calls=%fused_computation.75 | convolution fusion | flops 11814043648 | bytes 19922944 | tf_op jit(solution)/shard_map/dot_general | solution.py:131
  737.2 17.2 %convolution_convert_fusion.2 = bf16[2048,1408]{1,0:T(8,128)(2,1)S(1)} fusion(bf16[2048,2048]{1,0:T(8,128)(2,1)} %all-gather.9.cloned.1.call-done, bf16[2048,1408]{0,1:T(8,128)(2,1)} %get-tuple-element.446), kind=kOutput, calls=%fused_computation.77 | convolution fusion | flops 11814043648 | bytes 19922944 | tf_op jit(solution)/shard_map/dot_general | solution.py:131
  790.1 17.6 %convolution_convert_fusion.3 = bf16[2048,1408]{1,0:T(8,128)(2,1)S(1)} fusion(bf16[2048,2048]{1,0:T(8,128)(2,1)} %all-gather.9.cloned.1.call-done, bf16[2048,1408]{0,1:T(8,128)(2,1)} %get-tuple-element.445), kind=kOutput, calls=%fused_computation.78 | convolution fusion | flops 11814043648 | bytes 19922944 | tf_op jit(solution)/shard_map/dot_general | solution.py:131
  890.4 28.6 %collective-permute-done.31 = bf16[128,2048]{1,0:T(8,128)(2,1)S(1)} collective-permute-done((bf16[128,2048]{1,0:T(8,128)(2,1)S(1)}, bf16[128,2048]{1,0:T(8,128)(2,1)S(1)}, u32[]{:S(2)}, u32[]{:S(2)}) %collective-permute-start.31) | collective-permute-done | bytes 524320 | tf_op jit(solution)/shard_map/ppermute | solution.py:36
  934.2 52.3 %while.33 = (s32[]{:T(128)}, f32[1024,4,128]{0,2,1:T(8,128)S(1)}, f32[1024,4,128]{0,2,1:T(8,128)}, bf16[2,512,4,128]{3,2,1,0:T(4,128)(2,1)}, s32[2]{0:T(128)S(1)...) while((s32[]{:T(128)}, f32[1024,4,128]{0,2,1:T(8,128)S(1)}, ...), condition=%wide.region_22.23_spmd.clone.clone, body=%wide.region_20.22_spmd.clone.clone.sunk | while | flops 2720005632 | bytes 189332000 | solution.py:265
  1047.2 24.3 %collective-permute-done.61 = bf16[512,1408]{1,0:T(8,128)(2,1)} collective-permute-done((bf16[512,1408]{1,0:T(8,128)(2,1)}, bf16[512,1408]{1,0:T(8,128)(2,1)}, u32[]{:S(2)}, u32[]{:S(2)}) %collective-permute-start.61) | collective-permute-done | bytes 1441824 | tf_op jit(solution)/shard_map/ppermute | solution.py:36
  1081.0 24.2 %collective-permute-done.49 = bf16[1,8,2,64,768]{4,3,2,1,0:T(8,128)(2,1)} collective-permute-done((bf16[1,8,2,64,768]{4,3,2,1,0:T(8,128)(2,1)}, bf16[1,8,2,64,768]{4,3,2,1,0:T(8,128)(2,1)}, u32[]{:S(2)}, u32[]{:S(2)}) %collective-permute-start.49) | collective-permute-done | bytes 1572896 | tf_op jit(solution)/shard_map/ppermute | solution.py:36
  1109.0 34.0 %collective-permute-done.41 = f32[10,2048]{1,0:T(8,128)S(1)} collective-permute-done((f32[10,2048]{1,0:T(8,128)S(1)}, f32[10,2048]{1,0:T(8,128)S(1)}, u32[]{:S(2)}, u32[]{:S(2)}) %collective-permute-start.41) | collective-permute-done | bytes 81952 | tf_op jit(solution)/shard_map/ppermute | solution.py:36
  1169.7 19.6 %all-to-all-done.6 = bf16[8,2,64,768]{3,2,1,0:T(8,128)(2,1)S(1)} async-done(((bf16[8,2,64,768]{3,2,1,0:T(8,128)(2,1)}), bf16[8,2,64,768]{3,2,1,0:T(8,128)(2,1)S(1)}, u32[]{:S(2)}, u32[]{:S(2)}) %all-to-all-start.6) | async-done | bytes 1572896 | tf_op jit(solution)/shard_map/all_to_all | solution.py:110
  (661 shorter events, 753.9 us)
Async XLA Ops:
  7.2 70.5 %all-gather.5.cloned.1.call-start = ((), (), s32[]{:S(2)}) async-start(), calls=%async_computation.14 | async-start | bytes 7077888 | tf_op jit(solution)/shard_map/all_gather | solution.py:100
  9.4 114.9 %all-gather.7.cloned.1.call-start = ((), (), s32[]{:S(2)}) async-start(), calls=%async_computation.15 | async-start | bytes 2359296 | tf_op jit(solution)/shard_map/all_gather | solution.py:303
  43.0 409.0 %all-gather.9.cloned.1.call-start = ((), (), s32[]{:S(2)}) async-start(), calls=%async_computation.16 | async-start | bytes 9437184 | tf_op jit(solution)/shard_map/all_gather | solution.py:100
  226.0 85.4 %collective-permute-start.16 = (bf16[1408,512]{1,0:T(8,128)(2,1)}, bf16[1408,512]{1,0:T(8,128)(2,1)S(1)}, u32[]{:S(2)}, u32[]{:S(2)}) collective-permute-start(bf16[1408,512]{1,0:T(8,128)(2,1)} %bitcast.287), channel_id=1, source_target_pairs={{0,2},{1,3},{2,0},{3,1},{4,6},{5,7},{6,4},{7,5},{8,10},{9,11},{10,... | collective-permute-start | bytes 4325384 | tf_op jit(solution)/shard_map/ppermute | solution.py:36
  249.8 70.8 %collective-permute-start.18 = (bf16[1408,512]{1,0:T(8,128)(2,1)}, bf16[1408,512]{1,0:T(8,128)(2,1)}, u32[]{:S(2)}, u32[]{:S(2)}) collective-permute-start(bf16[1408,512]{1,0:T(8,128)(2,1)} %bitcast.288), channel_id=1, source_target_pairs={{0,1},{1,0},{2,3},{3,2},{4,5},{5,4},{6,7},{7,6},{8,9},{9,8},{10,11... | collective-permute-start | bytes 4325384 | tf_op jit(solution)/shard_map/ppermute | solution.py:36
  264.4 100.4 %all-to-all-start.2 = ((bf16[8,2,64,768]{3,2,1,0:T(8,128)(2,1)}), bf16[8,2,64,768]{3,2,1,0:T(8,128)(2,1)S(1)}, u32[]{:S(2)}, u32[]{:S(2)}) async-start(bf16[8,2,64,768]{3,2,1,0:T(8,128)(2,1)} %bitcast.12), calls=%async_computation.2 | async-start | bytes 3145728 | tf_op jit(solution)/shard_map/all_to_all | solution.py:110
  268.0 221.8 %all-gather.11.cloned.1.call-start = ((), (), s32[]{:S(2)}) async-start(), calls=%async_computation.18 | async-start | bytes 9437184 | tf_op jit(solution)/shard_map/all_gather | solution.py:100
  555.9 271.2 %reduce-scatter.7.cloned.1.call-start = ((), (), s32[]{:S(2)}) async-start(), calls=%async_computation.19 | async-start | bytes 9437184 | tf_op jit(solution)/shard_map/reduce_scatter | solution.py:104
  669.6 177.1 %reduce-scatter.5.cloned.1.call-start = ((), (), s32[]{:S(2)}) async-start(), calls=%async_computation.17 | async-start | bytes 9437184 | tf_op jit(solution)/shard_map/reduce_scatter | solution.py:104
  717.0 539.3 %reduce-scatter.11.cloned.1.call-start = ((), (), s32[]{:S(2)}) async-start(), calls=%async_computation.21 | async-start | bytes 2359296 | tf_op jit(solution)/shard_map/reduce_scatter | solution.py:104
  735.2 85.7 %collective-permute-start.62 = (bf16[704,512]{1,0:T(8,128)(2,1)}, bf16[704,512]{1,0:T(8,128)(2,1)}, u32[]{:S(2)}, u32[]{:S(2)}) collective-permute-start(bf16[704,512]{1,0:T(8,128)(2,1)} %get-tuple-element.463), channel_id=1, source_target_pairs={{0,1},{1,0},{2,3},{3,2},{4,5},{5,4},{6,7},{7,6},{8,9},{9,8},{10,11... | collective-permute-start | bytes 2162696 | tf_op jit(solution)/shard_map/ppermute | solution.py:36
  735.7 86.7 %collective-permute-start.64 = (bf16[704,512]{1,0:T(8,128)(2,1)}, bf16[704,512]{1,0:T(8,128)(2,1)}, u32[]{:S(2)}, u32[]{:S(2)}) collective-permute-start(bf16[704,512]{1,0:T(8,128)(2,1)} %get-tuple-element.465), channel_id=1, source_target_pairs={{0,2},{1,3},{2,0},{3,1},{4,6},{5,7},{6,4},{7,5},{8,10},{9,11},{10,... | collective-permute-start | bytes 2162696 | tf_op jit(solution)/shard_map/ppermute | solution.py:36
  756.1 94.9 %collective-permute-start.58 = (bf16[256,1408]{1,0:T(8,128)(2,1)}, bf16[256,1408]{1,0:T(8,128)(2,1)}, u32[]{:S(2)}, u32[]{:S(2)}) collective-permute-start(bf16[256,1408]{1,0:T(8,128)(2,1)} %get-tuple-element.469), channel_id=1, source_target_pairs={{0,1},{1,0},{2,3},{3,2},{4,5},{5,4},{6,7},{7,6},{8,9},{9,8},{10,11... | collective-permute-start | bytes 2162696 | tf_op jit(solution)/shard_map/ppermute | solution.py:36
  822.5 183.4 %collective-permute-start.46 = (bf16[1,4,2,64,768]{4,3,2,1,0:T(8,128)(2,1)}, bf16[1,4,2,64,768]{4,3,2,1,0:T(8,128)(2,1)}, u32[]{:S(2)}, u32[]{:S(2)}) collective-permute-start(bf16[1,4,2,64,768]{4,3,2,1,0:T(8,128)(2,1)} %get-tuple-element.527), channel_id=1, source_target_pairs={{0,1},{1,0},{2,3},{3,2},{4,5},{5,4},{6,7},{7,6},{8,9},{9,8},{10,11... | collective-permute-start | bytes 2359304 | tf_op jit(solution)/shard_map/ppermute | solution.py:36
  856.0 153.9 %collective-permute-start.48 = (bf16[1,4,2,64,768]{4,3,2,1,0:T(8,128)(2,1)}, bf16[1,4,2,64,768]{4,3,2,1,0:T(8,128)(2,1)}, u32[]{:S(2)}, u32[]{:S(2)}) collective-permute-start(bf16[1,4,2,64,768]{4,3,2,1,0:T(8,128)(2,1)} %get-tuple-element.528), channel_id=1, source_target_pairs={{0,2},{1,3},{2,0},{3,1},{4,6},{5,7},{6,4},{7,5},{8,10},{9,11},{10,... | collective-permute-start | bytes 2359304 | tf_op jit(solution)/shard_map/ppermute | solution.py:36
  856.7 156.5 %collective-permute-start.51 = (bf16[192,2048]{1,0:T(8,128)(2,1)}, bf16[192,2048]{1,0:T(8,128)(2,1)}, u32[]{:S(2)}, u32[]{:S(2)}) collective-permute-start(bf16[192,2048]{1,0:T(8,128)(2,1)} %pad_maximum_fusion.29), channel_id=1, source_target_pairs={{0,2},{1,3},{2,0},{3,1},{4,6},{5,7},{6,4},{7,5},{8,10},{9,11},{10,... | collective-permute-start | bytes 2359304 | tf_op jit(solution)/shard_map/ppermute | solution.py:36
  888.9 124.8 %collective-permute-start.53 = (bf16[192,2048]{1,0:T(8,128)(2,1)}, bf16[192,2048]{1,0:T(8,128)(2,1)}, u32[]{:S(2)}, u32[]{:S(2)}) collective-permute-start(bf16[192,2048]{1,0:T(8,128)(2,1)} %pad_maximum_fusion.30), channel_id=1, source_target_pairs={{0,1},{1,0},{2,3},{3,2},{4,5},{5,4},{6,7},{7,6},{8,9},{9,8},{10,11... | collective-permute-start | bytes 2359304 | tf_op jit(solution)/shard_map/ppermute | solution.py:36
  919.0 103.4 %collective-permute-start.63 = (bf16[1408,512]{1,0:T(8,128)(2,1)}, bf16[1408,512]{1,0:T(8,128)(2,1)}, u32[]{:S(2)}, u32[]{:S(2)}) collective-permute-start(bf16[1408,512]{1,0:T(8,128)(2,1)} %pad_maximum_fusion.14), channel_id=1, source_target_pairs={{0,2},{1,3},{2,0},{3,1},{4,6},{5,7},{6,4},{7,5},{8,10},{9,11},{10,... | collective-permute-start | bytes 4325384 | tf_op jit(solution)/shard_map/ppermute | solution.py:36
  926.6 331.5 %reduce-scatter.9.cloned.1.call-start = ((), (), s32[]{:S(2)}) async-start(), calls=%async_computation.20 | async-start | bytes 7077888 | tf_op jit(solution)/shard_map/reduce_scatter | solution.py:104
  1013.7 67.3 %collective-permute-start.47 = (bf16[1,8,2,64,768]{4,3,2,1,0:T(8,128)(2,1)}, bf16[1,8,2,64,768]{4,3,2,1,0:T(8,128)(2,1)}, u32[]{:S(2)}, u32[]{:S(2)}) collective-permute-start(bf16[1,8,2,64,768]{4,3,2,1,0:T(8,128)(2,1)} %pad_maximum_fusion.8), channel_id=1, source_target_pairs={{0,2},{1,3},{2,0},{3,1},{4,6},{5,7},{6,4},{7,5},{8,10},{9,11},{10,... | collective-permute-start | bytes 4718600 | tf_op jit(solution)/shard_map/ppermute | solution.py:36
  1022.4 82.8 %collective-permute-start.49 = (bf16[1,8,2,64,768]{4,3,2,1,0:T(8,128)(2,1)}, bf16[1,8,2,64,768]{4,3,2,1,0:T(8,128)(2,1)}, u32[]{:S(2)}, u32[]{:S(2)}) collective-permute-start(bf16[1,8,2,64,768]{4,3,2,1,0:T(8,128)(2,1)} %pad_maximum_fusion.9), channel_id=1, source_target_pairs={{0,1},{1,0},{2,3},{3,2},{4,5},{5,4},{6,7},{7,6},{8,9},{9,8},{10,11... | collective-permute-start | bytes 4718600 | tf_op jit(solution)/shard_map/ppermute | solution.py:36
  1040.6 124.7 %collective-permute-start.55 = (bf16[512,1408]{1,0:T(8,128)(2,1)}, bf16[512,1408]{1,0:T(8,128)(2,1)}, u32[]{:S(2)}, u32[]{:S(2)}) collective-permute-start(bf16[512,1408]{1,0:T(8,128)(2,1)} %pad_maximum_fusion.10), channel_id=1, source_target_pairs={{0,2},{1,3},{2,0},{3,1},{4,6},{5,7},{6,4},{7,5},{8,10},{9,11},{10,... | collective-permute-start | bytes 4325384 | tf_op jit(solution)/shard_map/ppermute | solution.py:36
  1045.6 119.7 %collective-permute-start.57 = (bf16[512,1408]{1,0:T(8,128)(2,1)}, bf16[512,1408]{1,0:T(8,128)(2,1)}, u32[]{:S(2)}, u32[]{:S(2)}) collective-permute-start(bf16[512,1408]{1,0:T(8,128)(2,1)} %pad_maximum_fusion.11), channel_id=1, source_target_pairs={{0,1},{1,0},{2,3},{3,2},{4,5},{5,4},{6,7},{7,6},{8,9},{9,8},{10,11... | collective-permute-start | bytes 4325384 | tf_op jit(solution)/shard_map/ppermute | solution.py:36
  1075.4 68.9 %all-to-all-start.9 = ((bf16[4,2,192,256]{3,2,1,0:T(8,128)(2,1)}), bf16[4,2,192,256]{3,2,1,0:T(8,128)(2,1)S(1)}, u32[]{:S(2)}, u32[]{:S(2)}) async-start(bf16[4,2,192,256]{3,2,1,0:T(8,128)(2,1)} %bitcast.50), calls=%async_computation.13 | async-start | bytes 1572864 | tf_op jit(solution)/shard_map/all_to_all | solution.py:110
  (194 other events, 4116.5 us)
Sparse Core Ops, SparseCore 0:
  10.2 67.4 all-gather.4
  79.3 29.2 all-gather.6
  181.1 104.1 all-gather.8
  291.3 86.9 all-gather.10
  669.7 86.7 reduce-scatter.6
  758.6 87.9 reduce-scatter.4
  926.7 35.5 reduce-scatter.10
  1003.5 81.8 reduce-scatter.8

commit v2 on v1

v2 whole, which is shorter than its diff:
```python
import functools

import jax
import jax.numpy as jnp
from jax import lax
from jax.experimental import pallas as pl
from jax.experimental.pallas import tpu as pltpu
from jax.sharding import PartitionSpec as P

DH = 128


EPS = 1e-06
CLIP_LIMIT = 6.0
NEG = -1e30
HIGH = lax.Precision.HIGHEST
CONTRACT_LAST = (((1,), (1,)), ((), ()))
CONTRACT_FIRST = (((0,), (0,)), ((), ()))


def norm_rows(inputs, gain):
    factor = lax.rsqrt(jnp.mean(inputs * inputs, axis=-1, keepdims=True) + EPS)
    return (inputs * factor * gain, factor)


def norm_back(inputs, factor, gain, upstream):
    scaled = upstream * gain
    inner = jnp.mean(scaled * inputs, axis=-1, keepdims=True)
    return (
        factor * scaled - inputs * (factor * factor * factor) * inner,
        jnp.sum(upstream * inputs * factor, axis=0),
    )


def pairs(count, bit):
    return [(index, index ^ bit) for index in range(count)]


def swap(values_in, bit, axis_name="tensor"):
    return lax.ppermute(values_in, axis_name, pairs(lax.axis_size(axis_name), bit))


def halves(values_in, axis):
    middle_at = values_in.shape[axis] // 2
    return (
        lax.slice_in_dim(values_in, 0, middle_at, axis=axis),
        lax.slice_in_dim(values_in, middle_at, values_in.shape[axis], axis=axis),
    )


def after(value, *others):
    return lax.optimization_barrier((value, others))[0]


def cut_of(block):
    return 1 if block.ndim > 2 else 0


def gather_near(block):
    if lax.axis_size("tensor") != 4:
        return (block,)
    return (block, swap(block, 1), swap(block, 2))


def gather_far(parts):
    if len(parts) == 1:
        return parts
    block, across, along = parts
    cut = cut_of(block)
    first, _ = halves(along, cut)
    _, second = halves(across, cut)
    return (block, across, along, swap(first, 1), swap(second, 2))


def gather_join(parts, axis):
    if len(parts) == 1:
        return lax.all_gather(parts[0], "tensor", axis=axis, tiled=True)
    block, across, along, first, second = parts
    diagonal = jnp.concatenate([first, second], axis=cut_of(block))
    here = lax.axis_index("tensor")
    odd, high = (here & 1) == 1, (here & 2) == 2
    low_even, low_odd = jnp.where(odd, across, block), jnp.where(odd, block, across)
    high_even, high_odd = jnp.where(odd, diagonal, along), jnp.where(odd, along, diagonal)
    return jnp.concatenate(
        [
            jnp.where(high, high_even, low_even),
            jnp.where(high, high_odd, low_odd),
            jnp.where(high, low_even, high_even),
            jnp.where(high, low_odd, high_odd),
        ],
        axis=axis,
    )


def block_of(partial, other, axis):
    size = partial.shape[axis] // 4
    return lax.dynamic_slice_in_dim(
        partial, (lax.axis_index("tensor") ^ other) * size, size, axis
    )


def scatter_far(partial, axis):
    if lax.axis_size("tensor") != 4:
        return (partial,)
    first, second = halves(block_of(partial, 3, axis), cut_of(partial))
    return (partial, swap(first, 1), swap(second, 2))


def scatter_ready(parts, axis):
    if len(parts) == 1:
        return parts
    partial, over_x, over_y = parts
    cut = cut_of(partial)
    wide = jnp.float32
    near_y, near_x = halves(block_of(partial, 2, axis), cut), halves(block_of(partial, 1, axis), cut)
    send_y = jnp.concatenate(
        [(near_y[0].astype(wide) + over_x.astype(wide)).astype(partial.dtype), near_y[1]], axis=cut
    )
    send_x = jnp.concatenate(
        [near_x[0], (near_x[1].astype(wide) + over_y.astype(wide)).astype(partial.dtype)], axis=cut
    )
    return (block_of(partial, 0, axis), send_y, send_x)


def scatter_send(parts, axis):
    if len(parts) == 1:
        return (lax.psum_scatter(parts[0], "tensor", scatter_dimension=axis, tiled=True),)
    block, send_y, send_x = parts
    return (block, swap(send_y, 2), swap(send_x, 1))


def scatter_near(parts, axis):
    return scatter_send(scatter_ready(parts, axis), axis)


def scatter_sum(parts):
    total = parts[0].astype(jnp.float32)
    for part in parts[1:]:
        total = total + part.astype(jnp.float32)
    return total


def column_gather(rows):
    return lax.all_gather(rows, "dp", axis=0, tiled=True)


def column_scatter(partial, axis):
    return lax.psum_scatter(
        partial.astype(jnp.bfloat16), "dp", scatter_dimension=axis, tiled=True
    ).astype(jnp.float32)


def trade(blocks, axis_name):
    return lax.all_to_all(blocks, axis_name, split_axis=0, concat_axis=0, tiled=True)


def butterfly(values_in, combine, axis_names):
    for axis_name in axis_names:
        bit = 1
        while bit < lax.axis_size(axis_name):
            values_in = combine(values_in, swap(values_in, bit, axis_name))
            bit *= 2
    return values_in


def times(left, right):
    return jnp.dot(left, right, preferred_element_type=jnp.float32)


def times_last(left, right):
    return lax.dot_general(left, right, CONTRACT_LAST, preferred_element_type=jnp.float32)


def times_first(left, right):
    return lax.dot_general(left, right, CONTRACT_FIRST, preferred_element_type=jnp.float32)


def slice_width(hidden_width, share):
    return -(-hidden_width // (128 * share)) * 128


def pack(blocks, width):
    *lead, rows, columns = blocks.shape
    groups = width // columns
    blocks = blocks.reshape(*lead, groups, rows // groups, columns)
    return jnp.swapaxes(blocks, -3, -2).reshape(*lead, rows // groups, width)


def unpack(blocks, columns):
    *lead, rows, width = blocks.shape
    groups = width // columns
    blocks = jnp.swapaxes(blocks.reshape(*lead, rows, groups, columns), -3, -2)
    return blocks.reshape(*lead, groups * rows, columns)


def shared_sizes(rows, hidden_width):
    count, owners = lax.axis_size("tensor"), lax.axis_size("dp")
    share = owners // count
    width = slice_width(hidden_width, share)
    return count, share, width, rows // count, width // count


def shared_spread(in_weights, out_weight):
    rows, hidden_width = in_weights[0].shape
    count, share, width, piece, slab = shared_sizes(rows, hidden_width)
    extra = share * width - hidden_width
    padded = [jnp.pad(w, ((0, 0), (0, extra))).reshape(count, piece, -1) for w in in_weights]
    first = jnp.stack(
        [
            jnp.concatenate([w[:, :, s * width : (s + 1) * width] for w in padded], axis=2)
            for s in range(share)
        ],
        axis=1,
    )
    last = jnp.pad(out_weight, ((0, extra), (0, 0)))
    last = pack(last.reshape(share, count, slab, -1).transpose(1, 0, 2, 3), 2 * width)
    return trade(jnp.concatenate([first, last], axis=2), "tensor")


def shared_owners(blocks):
    count, share, rows, width = blocks.shape
    return trade(blocks.reshape(count * share, rows, width), "dp")


def shared_join(whole, rows, columns):
    count, owners, _, width = whole.shape
    piece = rows // count
    first = whole[:, :, :piece].transpose(1, 0, 2, 3).reshape(owners * rows, width)
    last = unpack(whole[:, :, piece:], columns).transpose(0, 2, 1, 3)
    return first, last.reshape(-1, owners * columns)


def shared_back(grad_in, grad_out, columns):
    count, owners = lax.axis_size("tensor"), lax.axis_size("dp")
    rows, width = grad_in.shape
    first = grad_in.reshape(owners, count, rows // (owners * count), width).transpose(1, 0, 2, 3)
    last = grad_out.reshape(count, -1, owners, columns).transpose(0, 2, 1, 3)
    return jnp.concatenate([first, pack(last, width)], axis=2)


def shared_back_group(blocks, rows, columns, hidden_width):
    count, share, width, piece, slab = shared_sizes(rows, hidden_width)
    blocks = trade(blocks.reshape(count, share, -1, 2 * width), "tensor")
    first = blocks[:, :, :piece].reshape(count, share, piece, 2, width)
    first = [
        jnp.concatenate([first[:, s, :, part] for s in range(share)], axis=2)
        .reshape(rows, share * width)[:, :hidden_width]
        .astype(jnp.float32)
        for part in range(2)
    ]
    last = unpack(blocks[:, :, piece:], columns).transpose(1, 0, 2, 3).reshape(-1, columns)
    return first[0], first[1], last[:hidden_width].astype(jnp.float32)


def join_kernel(place_ref, *refs):
    count = (len(refs) - 2) // 5
    whole, sems = refs[-2:]
    here = place_ref[0]
    copies = []
    for side in range(count):
        parts = refs[5 * side : 5 * side + 5]
        rows, columns = parts[0].shape
        half = rows // 2
        for index, (part, other, shift) in enumerate(
            zip(parts, (0, 1, 2, 3, 3), (0, 0, 0, 0, half))
        ):
            start = pl.multiple_of((here ^ other) * rows + shift, half)
            copies.append(
                pltpu.make_async_copy(
                    part,
                    whole.at[pl.ds(start, part.shape[0]), pl.ds(side * columns, columns)],
                    sems.at[5 * side + index],
                )
            )
    for copy in copies:
        copy.start()
    for copy in copies:
        copy.wait()


def gather_rows(*gathers):
    if len(gathers[0]) == 1:
        return jnp.concatenate([gather_join(parts, 0) for parts in gathers], axis=1)
    rows, columns = gathers[0][0].shape
    shape = (4 * rows, len(gathers) * columns)
    operands = [part for parts in gathers for part in parts]
    return pl.pallas_call(
        join_kernel,
        grid_spec=pltpu.PrefetchScalarGridSpec(
            num_scalar_prefetch=1,
            grid=(1,),
            in_specs=[pl.BlockSpec(memory_space=pl.ANY)] * len(operands),
            out_specs=pl.BlockSpec(shape, lambda step, _: (0, 0)),
            scratch_shapes=[pltpu.SemaphoreType.DMA((len(operands),))],
        ),
        out_shape=jax.ShapeDtypeStruct(shape, operands[0].dtype),
        compiler_params=pltpu.CompilerParams(vmem_limit_bytes=40 << 20),
        name="join_rows",
    )(lax.axis_index("tensor").astype(jnp.int32).reshape(1), *operands)


def attention_scores(query_block, keys_in, start, length):
    rows, columns = query_block.shape[0], keys_in.shape[0]
    raw = lax.dot_general(
        query_block, keys_in, CONTRACT_LAST, preferred_element_type=jnp.float32
    ) * DH ** (-0.5)
    row = start + lax.broadcasted_iota(jnp.int32, (rows, columns), 0)
    column = lax.broadcasted_iota(jnp.int32, (rows, columns), 1)
    allowed = (column <= row) & (column < length)
    scores = jnp.where(allowed, raw, NEG)
    powers = jnp.exp(scores - jnp.max(scores, axis=1, keepdims=True))
    probs = powers * (1.0 / jnp.sum(powers, axis=1, keepdims=True))
    return (scores, row, probs)


def attention_forward_kernel(
    length_ref, query_ref, key_ref, value_ref, attended_ref, peak_ref, *, block_len
):
    length = length_ref[0]
    peak = jnp.full((1, 1), NEG, jnp.float32)
    for start in range(0, query_ref.shape[0], block_len):
        stop = start + block_len
        scores, row, probs = attention_scores(
            query_ref[start:stop, :], key_ref[:stop, :], start, length
        )
        attended_ref[start:stop, :] = jnp.dot(
            probs.astype(jnp.bfloat16), value_ref[:stop, :], preferred_element_type=jnp.float32
        ).astype(jnp.bfloat16)
        counted = jnp.where(row < length, scores, NEG)
        peak = jnp.maximum(
            peak, jnp.max(jnp.max(counted, axis=1, keepdims=True), axis=0, keepdims=True)
        )
    peak_ref[0] = jnp.broadcast_to(peak, peak_ref.shape[1:])


def attention_forward(projected, length):
    seq_len = projected.shape[0]
    heads = projected.shape[1] // (3 * DH)
    block_len = min(256, seq_len)

    def columns(part):
        return pl.BlockSpec((seq_len, DH), lambda head, _: (0, part * heads + head))

    attended, peaks = pl.pallas_call(
        functools.partial(attention_forward_kernel, block_len=block_len),
        grid_spec=pltpu.PrefetchScalarGridSpec(
            num_scalar_prefetch=1,
            grid=(heads,),
            in_specs=[columns(0), columns(1), columns(2)],
            out_specs=[
                pl.BlockSpec((seq_len, DH), lambda head, _: (0, head)),
                pl.BlockSpec((1, 8, 128), lambda head, _: (head, 0, 0)),
            ],
        ),
        out_shape=(
            jax.ShapeDtypeStruct((seq_len, heads * DH), jnp.bfloat16),
            jax.ShapeDtypeStruct((heads, 8, 128), jnp.float32),
        ),
        compiler_params=pltpu.CompilerParams(vmem_limit_bytes=48 << 20),
        cost_estimate=pl.CostEstimate(
            flops=6 * heads * seq_len * seq_len * DH,
            bytes_accessed=8 * heads * seq_len * DH,
            transcendentals=heads * seq_len * seq_len,
        ),
        name="attention_forward",
    )(length, projected, projected, projected)
    return (attended, peaks[:, 0, 0])


def attention_backward_kernel(
    length_ref, query_ref, key_ref, value_ref, grad_ref, out_ref, key_sum, value_sum, *, block_len
):
    part = pl.program_id(1)
    low, factor = jnp.bfloat16, DH ** (-0.5)

    @pl.when(part == 0)
    def _():
        length = length_ref[0]
        seq_len = query_ref.shape[0]
        for start in range(seq_len - block_len, -1, -block_len):
            stop = start + block_len
            query_block, grad_block = query_ref[start:stop, :], grad_ref[start:stop, :]
            keys_in = key_ref[:stop, :]
            _, _, probs = attention_scores(query_block, keys_in, start, length)
            along = lax.dot_general(
                grad_block, value_ref[:stop, :], CONTRACT_LAST, preferred_element_type=jnp.float32
            )
            inner = jnp.sum(probs * along, axis=1, keepdims=True)
            grad_scores = (probs * (along - inner)).astype(low)
            out_ref[start:stop, :] = (
                jnp.dot(grad_scores, keys_in, preferred_element_type=jnp.float32) * factor
            ).astype(low)
            key_part = lax.dot_general(
                grad_scores, query_block, CONTRACT_FIRST, preferred_element_type=jnp.float32
            )
            value_part = lax.dot_general(
                probs.astype(low), grad_block, CONTRACT_FIRST, preferred_element_type=jnp.float32
            )
            if stop == seq_len:
                key_sum[...] = key_part
                value_sum[...] = value_part
            else:
                key_sum[:stop, :] += key_part
                value_sum[:stop, :] += value_part

    @pl.when(part == 1)
    def _():
        out_ref[...] = (key_sum[...] * factor).astype(low)

    @pl.when(part == 2)
    def _():
        out_ref[...] = value_sum[...].astype(low)


def attention_backward(projected, grad_out, length):
    seq_len = projected.shape[0]
    heads = projected.shape[1] // (3 * DH)
    block_len = min(256, seq_len)

    def columns(part):
        return pl.BlockSpec((seq_len, DH), lambda head, _, __: (0, part * heads + head))

    return pl.pallas_call(
        functools.partial(attention_backward_kernel, block_len=block_len),
        grid_spec=pltpu.PrefetchScalarGridSpec(
            num_scalar_prefetch=1,
            grid=(heads, 3),
            in_specs=[
                columns(0),
                columns(1),
                columns(2),
                pl.BlockSpec((seq_len, DH), lambda head, _, __: (0, head)),
            ],
            out_specs=pl.BlockSpec((seq_len, DH), lambda head, part, _: (0, part * heads + head)),
            scratch_shapes=[
                pltpu.VMEM((seq_len, DH), jnp.float32),
                pltpu.VMEM((seq_len, DH), jnp.float32),
            ],
        ),
        out_shape=jax.ShapeDtypeStruct(projected.shape, jnp.bfloat16),
        compiler_params=pltpu.CompilerParams(vmem_limit_bytes=48 << 20),
        cost_estimate=pl.CostEstimate(
            flops=12 * heads * seq_len * seq_len * DH,
            bytes_accessed=14 * heads * seq_len * DH,
            transcendentals=heads * seq_len * seq_len,
        ),
        name="attention_backward",
    )(length, projected, projected, projected, grad_out)


def expert_backward_kernel(
    scale_ref,
    upstream_ref,
    *refs,
):
    low = jnp.bfloat16
    count = 2
    pre_refs, in_refs, out_refs = refs[:count], refs[count : 2 * count], refs[2 * count : 3 * count]
    grad_refs = refs[3 * count : 4 * count]
    hidden_refs = refs[4 * count : 5 * count]
    inner_ref, rows_ref = refs[5 * count :]
    upstream = upstream_ref[...]
    total = None
    inners = []
    for part in range(count):
        width = hidden_refs[part].shape[1]
        scale = scale_ref[:, part : part + 1]
        gate_pre = pre_refs[part][:, :width].astype(jnp.float32)
        up_pre = pre_refs[part][:, width:].astype(jnp.float32)
        raw = lax.dot_general(
            upstream, out_refs[part][...], CONTRACT_LAST, preferred_element_type=jnp.float32
        )
        sigma = 1.0 / (1.0 + jnp.exp(-gate_pre))
        activated = gate_pre * sigma
        hidden = activated * up_pre
        inners.append(jnp.sum(hidden * raw, axis=1, keepdims=True))
        scaled = raw * scale
        hidden_refs[part][...] = (hidden * scale).astype(low)
        grad_refs[part][:, :width] = (
            scaled * up_pre * (sigma * (1.0 + gate_pre * (1.0 - sigma)))
        ).astype(low)
        grad_refs[part][:, width:] = (scaled * activated).astype(low)
        rows = lax.dot_general(
            grad_refs[part][...], in_refs[part][...], CONTRACT_LAST, preferred_element_type=jnp.float32
        )
        total = rows if total is None else total + rows
    inner_ref[...] = jnp.concatenate(inners, axis=1)
    rows_ref[...] = total.astype(low)


def expert_backward(scales, upstream, pre, in_weights, out_weights):
    rows, model_width = upstream.shape
    block = min(256, rows)
    widths = [w.shape[0] for w in out_weights]
    low = jnp.bfloat16

    def tall(width):
        return pl.BlockSpec((block, width), lambda step: (step, 0))

    def whole(array):
        return pl.BlockSpec(array.shape, lambda step: (0, 0), pipeline_mode=pl.Buffered(1))

    outs = pl.pallas_call(
        expert_backward_kernel,
        grid=(rows // block,),
        in_specs=[tall(2), tall(model_width)]
        + [tall(2 * w) for w in widths]
        + [whole(w) for w in in_weights]
        + [whole(w) for w in out_weights],
        out_specs=[tall(2 * w) for w in widths]
        + [tall(w) for w in widths]
        + [tall(2), tall(model_width)],
        out_shape=[jax.ShapeDtypeStruct((rows, 2 * w), low) for w in widths]
        + [jax.ShapeDtypeStruct((rows, w), low) for w in widths]
        + [
            jax.ShapeDtypeStruct((rows, 2), jnp.float32),
            jax.ShapeDtypeStruct((rows, model_width), low),
        ],
        compiler_params=pltpu.CompilerParams(vmem_limit_bytes=60 << 20),
        cost_estimate=pl.CostEstimate(
            flops=6 * rows * model_width * sum(widths),
            bytes_accessed=2 * rows * (2 * model_width + 5 * sum(widths))
            + 6 * model_width * sum(widths),
            transcendentals=rows * sum(widths),
        ),
        name="expert_backward",
    )(scales, upstream, *pre, *in_weights, *out_weights)
    return outs[0:2], outs[2:4], outs[4], outs[5]


def local(
    tokens,
    lengths,
    routes,
    attn_gain,
    w_query,
    w_key,
    w_value,
    w_output,
    moe_gain,
    w_router,
    w_sigmoid,
    shared_gate,
    shared_up,
    shared_down,
    expert_gate,
    expert_up,
    expert_down,
    cotangent,
):
    low = jnp.bfloat16
    hold = lax.optimization_barrier
    inputs = tokens.astype(jnp.float32)
    normed, inv_one = norm_rows(inputs, attn_gain)
    width = w_query.shape[1]
    hidden_width = expert_gate.shape[2]
    shared_shape = (shared_gate.shape[0], shared_down.shape[1], shared_gate.shape[1])
    in_weights = column_gather(jnp.concatenate([w_query, w_key, w_value], axis=1))
    out_weight = lax.all_gather(w_output, "dp", axis=1, tiled=True)
    upstream_column = column_gather(cotangent)
    normed_parts = gather_far(gather_near(normed.astype(low)))
    shared_blocks = shared_spread((shared_gate, shared_up), shared_down)
    normed_parts, expert_gate = hold((normed_parts, expert_gate))
    gathered_one = gather_join(normed_parts, 0)
    gate_parts = gather_near(expert_gate[0])
    projected = times(gathered_one, in_weights).astype(low)
    projected, shared_blocks, gate_parts, expert_up = hold(
        (projected, shared_blocks, gate_parts, expert_up)
    )
    up_parts = gather_near(expert_up[0])
    shared_blocks = shared_owners(shared_blocks)[None]
    attended, peaks = attention_forward(projected, lengths)
    middle_parts = scatter_near(scatter_far(times(attended, out_weight).astype(low), 0), 0)
    middle_parts, gate_parts, up_parts, shared_blocks, peaks = hold(
        (middle_parts, gate_parts, up_parts, shared_blocks, peaks)
    )
    gate_parts, up_parts = gather_far(gate_parts), gather_far(up_parts)
    middle = inputs + scatter_sum(middle_parts)
    moe_norm, inv_two = norm_rows(middle, moe_gain)
    moe_low, shared_blocks, peaks = hold((moe_norm.astype(low), shared_blocks, peaks))
    column = column_gather(moe_low)
    gate_parts, up_parts, expert_down, shared_blocks = hold(
        (gate_parts, up_parts, expert_down, shared_blocks)
    )
    shared_parts = gather_near(shared_blocks)
    down_parts = gather_near(expert_down[0])
    full_in = gather_rows(gate_parts, up_parts)
    moe_wide = moe_low.astype(jnp.float32)
    experts = w_router.shape[1]
    owners = lax.axis_size("dp")
    rows_dev, route_count = routes.shape
    column_rows = owners * rows_dev
    logits = jnp.dot(moe_wide, w_router, precision=HIGH)
    picked = (routes[:, :, None] == jnp.arange(experts, dtype=jnp.int32)[None, None, :]).astype(
        jnp.float32
    )
    chosen = jnp.sum(picked * logits[:, None, :], axis=2)
    gates = jax.nn.softmax(chosen, axis=1)
    mixing = jax.nn.sigmoid(jnp.dot(moe_wide, w_sigmoid, precision=HIGH))
    gate_of = jnp.sum(picked * gates[:, :, None], axis=1)
    scales = jnp.stack([gate_of.T, jnp.broadcast_to(mixing[None], (experts, rows_dev))], axis=1)
    scales = trade(scales, "dp").transpose(0, 2, 1).reshape(column_rows, 2)
    peaks = butterfly(peaks, jnp.maximum, ("dp",))
    column, full_in, scales, peaks, shared_parts = hold(
        (column, full_in, scales, peaks, shared_parts)
    )
    shared_parts = gather_far(shared_parts)
    pre_e = times(column, full_in).astype(low)
    pre_e, shared_parts, down_parts = hold((pre_e, shared_parts, down_parts))
    down_parts = gather_far(down_parts)
    part_in, part_down = shared_join(gather_join(shared_parts, 0), *shared_shape[:2])
    full_down = gather_join(down_parts, 1)
    pre_s = times(column, part_in).astype(low)
    (d_pre_e, d_pre_s), (hidden_e, hidden_s), inner, d_rows = expert_backward(
        scales, upstream_column, (pre_e, pre_s), (full_in, part_in), (full_down, part_down)
    )
    d_moe = column_scatter(d_rows, 0)
    inner = trade(inner.reshape(owners, rows_dev, 2).transpose(0, 2, 1), "dp")
    grad_down_e = times_first(hidden_e, upstream_column).astype(low)
    grad_down_e, d_pre_s, hidden_s = hold((grad_down_e, d_pre_s, hidden_s))
    back_down_e = scatter_far(grad_down_e, 1)
    grad_down_s = times_first(hidden_s, upstream_column).astype(low)
    grad_in_s = times_first(column, d_pre_s).astype(low)
    back_down_e, grad_down_s, grad_in_s, hidden_e, hidden_s = hold(
        (back_down_e, grad_down_s, grad_in_s, hidden_e, hidden_s)
    )
    back_down_e = scatter_near(back_down_e, 1)
    grads_s = shared_back(grad_in_s, grad_down_s, shared_shape[1])
    hidden_e, hidden_s, grads_s = hold((hidden_e, hidden_s, grads_s))
    back_s = scatter_far(grads_s, 0)
    routed_rows = (times(hidden_e, full_down) + times(hidden_s, part_down)).astype(low)
    routed_rows, back_s, inner, back_down_e = hold((routed_rows, back_s, inner, back_down_e))
    routed = column_scatter(routed_rows, 0)
    upstream = cotangent.astype(jnp.float32)
    d_mixing = mixing * (1.0 - mixing) * jnp.sum(inner[:, 1], axis=0)
    d_gates = jnp.sum(picked * inner[:, 0].T[:, None, :], axis=2)
    d_chosen = gates * (d_gates - jnp.sum(gates * d_gates, axis=1, keepdims=True))
    d_logits = jnp.sum(picked * d_chosen[:, :, None], axis=1)
    d_router_part = jnp.dot(d_logits.T, moe_wide, precision=HIGH)
    d_sigmoid_part = jnp.dot(d_mixing, moe_wide, precision=HIGH)
    d_moe = (
        d_moe
        + jnp.dot(d_logits, w_router.T, precision=HIGH)
        + d_mixing[:, None] * w_sigmoid[None, :]
    )
    d_middle_norm, d_moe_gain_part = norm_back(middle, inv_two, moe_gain, d_moe)
    d_middle = upstream + d_middle_norm
    d_middle_low, back_s, d_pre_e = hold((d_middle.astype(low), back_s, d_pre_e))
    whole_parts = gather_near(d_middle_low)
    back_s = scatter_ready(back_s, 0)
    whole_parts, back_s = hold((whole_parts, back_s))
    whole_parts = gather_far(whole_parts)
    whole_parts, back_s = hold((whole_parts, back_s))
    back_s = scatter_send(back_s, 0)
    whole_middle = gather_join(whole_parts, 0)
    d_attended = times_last(whole_middle, out_weight).astype(low)
    d_projected = attention_backward(projected, d_attended, lengths)
    small_parts = jnp.concatenate(
        [d_router_part, d_sigmoid_part[None], d_moe_gain_part[None]], axis=0
    )
    d_w_output = column_scatter(times_first(attended, whole_middle), 1)
    d_normed_rows = times_last(d_projected, in_weights).astype(low)
    d_normed_rows, d_projected, small_parts = hold((d_normed_rows, d_projected, small_parts))
    normed_parts = scatter_far(d_normed_rows, 0)
    d_in_weights = column_scatter(times_first(gathered_one, d_projected), 0)
    normed_parts, back_s, d_pre_e, back_down_e = hold(
        (normed_parts, back_s, d_pre_e, back_down_e)
    )
    normed_parts = scatter_near(normed_parts, 0)
    back_s = trade(scatter_sum(back_s).astype(low)[0], "dp")
    grad_gate_up = times_first(column, d_pre_e).astype(low)
    normed_parts, grad_gate_up = hold((normed_parts, grad_gate_up))
    d_expert_down = scatter_sum(back_down_e)
    back_gate_up = scatter_ready(scatter_far(grad_gate_up, 0), 0)
    d_normed = scatter_sum(normed_parts)
    d_inputs_norm, d_attn_gain_part = norm_back(inputs, inv_one, attn_gain, d_normed)
    small_sums = butterfly(
        jnp.concatenate([small_parts, d_attn_gain_part[None]], axis=0), jnp.add, ("tensor",)
    )
    back_gate_up, d_expert_down, small_sums, routed = hold(
        (back_gate_up, d_expert_down, small_sums, routed)
    )
    back_gate_up = scatter_send(back_gate_up, 0)
    d_tokens = d_middle + d_inputs_norm
    small_sums = butterfly(small_sums, jnp.add, ("dp",))
    d_attn_gain = small_sums[experts + 2]
    d_shared_gate, d_shared_up, d_shared_down = shared_back_group(back_s, *shared_shape)
    d_expert_in = scatter_sum(back_gate_up)
    clip_scale = jnp.sqrt(CLIP_LIMIT / jnp.maximum(peaks, CLIP_LIMIT))
    columns = jnp.repeat(clip_scale, DH)
    query_clipped = (w_query.astype(jnp.float32) * columns[None, :]).astype(low)
    key_clipped = (w_key.astype(jnp.float32) * columns[None, :]).astype(low)
    return (
        (middle + routed).astype(low),
        d_tokens,
        d_attn_gain,
        d_in_weights[:, :width],
        d_in_weights[:, width : 2 * width],
        d_in_weights[:, 2 * width :],
        d_w_output,
        small_sums[experts + 1],
        small_sums[:experts].T,
        small_sums[experts],
        d_shared_gate,
        d_shared_up,
        d_shared_down,
        d_expert_in[None, :, :hidden_width],
        d_expert_in[None, :, hidden_width:],
        d_expert_down[None],
        clip_scale,
        query_clipped,
        key_clipped,
    )


def solution(mesh):
    placed = (
        P(("dp", "tensor"), None),
        P("dp"),
        P(("dp", "tensor"), None),
        P(),
        P("dp", "tensor"),
        P("dp", "tensor"),
        P("dp", "tensor"),
        P("tensor", "dp"),
        P(),
        P(),
        P(),
        P("dp", "tensor"),
        P("dp", "tensor"),
        P("tensor", "dp"),
        P("dp", "tensor", None),
        P("dp", "tensor", None),
        P("dp", None, "tensor"),
        P(("dp", "tensor"), None),
    )
    return jax.shard_map(
        local,
        mesh=mesh,
        in_specs=placed,
        out_specs=(
            P(("dp", "tensor"), None),
            P(("dp", "tensor"), None),
            P(),
            P("dp", "tensor"),
            P("dp", "tensor"),
            P("dp", "tensor"),
            P("tensor", "dp"),
            P(),
            P(),
            P(),
            P("dp", "tensor"),
            P("dp", "tensor"),
            P("tensor", "dp"),
            P("dp", "tensor", None),
            P("dp", "tensor", None),
            P("dp", None, "tensor"),
            P("tensor"),
            P("dp", "tensor"),
            P("dp", "tensor"),
        ),
        check_vma=False,
    )
```

time: 1280 us -> 980 us (0.77)
  waiting for transfers between devices: 494 us -> 324 us
  matrix products: 378 us -> 210 us
  Pallas kernels: 0 us -> 126 us
  other arithmetic: 163 us -> 86.5 us
  local copies, waits for them, and re-layouts: 78.2 us -> 118 us
  starting transfers between devices: 122 us -> 89.5 us
    pallas_call x0 -> x4, Pallas kernels: none -> 126 us  [the longest x1 90.2 us: expert_backward(): pl.pallas_call(expert_backward_kernel, grid=(rows // block,), in_specs=[t...]
    dot_general x8 -> x2, matrix products: 123 us -> 13.8 us  [times_last(): lax.dot_general(left, right, CONTRACT_LAST, preferred_element_type=jnp.fl...]
    ppermute x69 -> x52, waiting for transfers between devices: 389 us -> 315 us  [swap(): lax.ppermute(values_in, axis_name, pairs(lax.axis_size(axis_name), bit))]
    all_to_all x9 -> x6, waiting for transfers between devices: 70.8 us -> 6.47 us  [trade(): lax.all_to_all(blocks, axis_name, split_axis=0, concat_axis=0, tiled=True)]
    convert_element_type x20 -> x12, other arithmetic: 63.5 us -> 18.1 us  [the longest x5 8.14 us: scatter_ready(): (near_x[1].astype(wide) + over_y.astype(wide)).astype(partial.dtype)]
    dot_general x14 -> x0, matrix products: 41.1 us -> none  [the longest x2 9.29 us: one_block(): jnp.einsum('hqk,qhd->khd', weights, grad_block, preferred_element_type=jn...]
    ppermute x69 -> x52, starting transfers between devices: 82.4 us -> 60.9 us  [swap(): lax.ppermute(values_in, axis_name, pairs(lax.axis_size(axis_name), bit))]
    unnamed x230 -> x186, local copies, waits for them, and re-layouts: 17.3 us -> 37.5 us
  transfers between devices with their start and end apart: 86 -> 66, of which waited for: 45 -> 36; matrix products, arithmetic and copies ran while one was open for 34% -> 38% of each run, Pallas kernels for 0% -> 4%
where the time goes in v2:
time: 980 us; the launch traced here: 971 us
  waiting for transfers between devices  324 us (33%)
  matrix products  210 us (21%)
  Pallas kernels  126 us (13%)
  local copies, waits for them, and re-layouts  118 us (12%)
  starting transfers between devices  89.5 us (9%)
  other arithmetic  86.5 us (9%)
  between operations  16.5 us (2%)
    ppermute x52, waiting for transfers between devices, swap(): lax.ppermute(values_in, axis_name, pairs(lax.axis_size(axis_name), bit))  315 us
    dot_general x6, matrix products, times(): return jnp.dot(left, right, preferred_element_type=jnp.float32)  97.5 us
    pallas_call x1, Pallas kernels, expert_backward(): pl.pallas_call(expert_backward_kernel, grid=(rows // block,), in_specs=[t...  90.2 us
    dot_general x6, matrix products, times_first(): lax.dot_general(left, right, CONTRACT_FIRST, preferred_element_type=jnp.f...  89.8 us
    ppermute x52, starting transfers between devices, swap(): lax.ppermute(values_in, axis_name, pairs(lax.axis_size(axis_name), bit))  60.9 us
    unnamed x186, local copies, waits for them, and re-layouts  37.5 us
    all_to_all x6, starting transfers between devices, trade(): lax.all_to_all(blocks, axis_name, split_axis=0, concat_axis=0, tiled=True)  27.2 us
  transfers between devices with their start and end apart: 66, of which 36 were waited for; matrix products, arithmetic and copies ran while one was open for 38% of the time, Pallas kernels for 4%

profile of v2, /device:TPU:0, one launch (start us, length us, event | category | flops | bytes accessed | tf_op | source)
XLA Modules:
  0.0 971.2 jit_solution(8287015533450248638)
XLA Ops:
  21.0 16.0 %collective-permute-done.1 = bf16[256,2048]{1,0:T(8,128)(2,1)} collective-permute-done((bf16[256,2048]{1,0:T(8,128)(2,1)S(1)}, bf16[256,2048]{1,0:T(8,128)(2,1)}, u32[]{:S(2)}, u32[]{:S(2)}) %collective-permute-start.1) | collective-permute-done | bytes 1048608 | tf_op jit(solution)/shard_map/ppermute | solution.py:40
  52.4 16.0 %collective-permute-done.3 = bf16[128,2048]{1,0:T(8,128)(2,1)S(1)} collective-permute-done((bf16[128,2048]{1,0:T(8,128)(2,1)S(1)}, bf16[128,2048]{1,0:T(8,128)(2,1)S(1)}, u32[]{:S(2)}, u32[]{:S(2)}) %collective-permute-start.3) | collective-permute-done | bytes 524320 | tf_op jit(solution)/shard_map/ppermute | solution.py:40
  77.7 12.5 %convolution_convert_fusion.7.query_ref.key_ref.value_ref = bf16[1024,1536]{1,0:T(8,128)(2,1)} fusion(bf16[2048,1536]{1,0:T(8,128)(2,1)} %all-gather.5.cloned.1.call-done, bf16[256,2048]{1,0:T(8,128)(2,1)} %get-tuple-element.324, bf16[256,2048]{1,0:T(8,128)(2,1)} %get-tuple-element.323, bf16[256,2048]{1,0:T(8,128)(2,1)} %get-tuple-element.322, ...), kind=kOutput, calls=%fused_computation.22 | convolution fusion | flops 6460801024 | bytes 13631488 | tf_op jit(solution)/shard_map/dot_general | solution.py:167
  90.2 17.2 %collective-permute-done.4.refs_1_ = bf16[512,1408]{1,0:T(8,128)(2,1)S(1)} collective-permute-done((bf16[512,1408]{1,0:T(8,128)(2,1)}, bf16[512,1408]{1,0:T(8,128)(2,1)S(1)}, u32[]{:S(2)}, u32[]{:S(2)}) %collective-permute-start.4) | collective-permute-done | bytes 1441824 | tf_op jit(solution)/shard_map/ppermute | solution.py:40
  117.4 10.3 %attention_forward.1 = (bf16[1024,512]{1,0:T(8,128)(2,1)S(1)}, f32[4,8,128]{2,1,0:T(8,128)S(1)}) custom-call(s32[1]{0:T(128)S(6)} %copy.135.length_ref, bf16[1024,1536]{1,0:T(8,128)(2,1)S(1)} %copy-done.10, bf16[1024,1536]{1,0:T(8,128)(2,1)S(1)} %copy-done.10, bf16[1024,1536]{1,0:T(8,128)(2,1)S(1)} %copy-done.10), custom_call_target="tpu_custom_call" | custom-call | flops 3221225472 | bytes 4194304 | tf_op jit(solution)/shard_map/attention_forward/pallas_call | solution.py:344
  140.3 11.1 %collective-permute-done.6 = bf16[128,2048]{1,0:T(8,128)(2,1)} collective-permute-done((bf16[128,2048]{1,0:T(8,128)(2,1)}, bf16[128,2048]{1,0:T(8,128)(2,1)}, u32[]{:S(2)}, u32[]{:S(2)}) %collective-permute-start.6) | collective-permute-done | bytes 524320 | tf_op jit(solution)/shard_map/ppermute | solution.py:40
  161.4 20.9 %collective-permute-done.10.refs_6_ = bf16[512,1408]{1,0:T(8,128)(2,1)} collective-permute-done((bf16[512,1408]{1,0:T(8,128)(2,1)}, bf16[512,1408]{1,0:T(8,128)(2,1)}, u32[]{:S(2)}, u32[]{:S(2)}) %collective-permute-start.10) | collective-permute-done | bytes 1441824 | tf_op jit(solution)/shard_map/ppermute | solution.py:40
  182.8 21.4 %collective-permute-done.9 = bf16[256,2048]{1,0:T(8,128)(2,1)} collective-permute-done((bf16[256,2048]{1,0:T(8,128)(2,1)}, bf16[256,2048]{1,0:T(8,128)(2,1)}, u32[]{:S(2)}, u32[]{:S(2)}) %collective-permute-start.9) | collective-permute-done | bytes 1048608 | tf_op jit(solution)/shard_map/ppermute | solution.py:40
  216.8 12.3 %collective-permute-done.12.refs_3_ = bf16[256,1408]{1,0:T(8,128)(2,1)S(1)} collective-permute-done((bf16[256,1408]{1,0:T(8,128)(2,1)S(1)}, bf16[256,1408]{1,0:T(8,128)(2,1)S(1)}, u32[]{:S(2)}, u32[]{:S(2)}) %collective-permute-start.12) | collective-permute-done | bytes 720928 | tf_op jit(solution)/shard_map/ppermute | solution.py:40
  231.6 11.3 %collective-permute-done.14.refs_8_ = bf16[256,1408]{1,0:T(8,128)(2,1)S(1)} collective-permute-done((bf16[256,1408]{1,0:T(8,128)(2,1)S(1)}, bf16[256,1408]{1,0:T(8,128)(2,1)S(1)}, u32[]{:S(2)}, u32[]{:S(2)}) %collective-permute-start.14) | collective-permute-done | bytes 720928 | tf_op jit(solution)/shard_map/ppermute | solution.py:40
  284.6 15.0 %collective-permute-done.19 = bf16[1,8,96,1536]{3,2,1,0:T(8,128)(2,1)} collective-permute-done((bf16[1,8,96,1536]{3,2,1,0:T(8,128)(2,1)}, bf16[1,8,96,1536]{3,2,1,0:T(8,128)(2,1)}, u32[]{:S(2)}, u32[]{:S(2)}) %collective-permute-start.19) | collective-permute-done | bytes 2359328 | tf_op jit(solution)/shard_map/ppermute | solution.py:40
  306.1 31.1 %convolution_convert_fusion.1.refs_0_ = bf16[2048,2816]{1,0:T(8,128)(2,1)} fusion(bf16[2048,2048]{1,0:T(8,128)(2,1)} %all-gather.9.cloned.1.call-done, bf16[2048,2816]{1,0:T(8,128)(2,1)} %join_rows.1.refs_2_), kind=kOutput, calls=%fused_computation.2 | convolution fusion | flops 23628087296 | bytes 31457280 | tf_op jit(solution)/shard_map/dot_general | solution.py:167
  337.3 15.7 %collective-permute-done.21 = bf16[1,4,96,1536]{3,2,1,0:T(8,128)(2,1)S(1)} collective-permute-done((bf16[1,4,96,1536]{3,2,1,0:T(8,128)(2,1)S(1)}, bf16[1,4,96,1536]{3,2,1,0:T(8,128)(2,1)S(1)}, u32[]{:S(2)}, u32[]{:S(2)}) %collective-permute-start.21) | collective-permute-done | bytes 1179680 | tf_op jit(solution)/shard_map/ppermute | solution.py:40
  369.6 19.0 %convolution_convert_fusion.3.refs_1_ = bf16[2048,1536]{1,0:T(8,128)(2,1)} fusion(bf16[2048,2048]{1,0:T(8,128)(2,1)} %all-gather.9.cloned.1.call-done, bf16[2048,1536]{1,0:T(8,128)(2,1)S(1)} %bitcast.133), kind=kOutput, calls=%fused_computation.6 | convolution fusion | flops 12888047616 | bytes 20971520 | tf_op jit(solution)/shard_map/dot_general | solution.py:167
  414.4 90.2 %expert_backward.1 = (bf16[2048,2816]{1,0:T(8,128)(2,1)}, bf16[2048,1536]{1,0:T(8,128)(2,1)}, bf16[2048,1408]{1,0:T(8,128)(2,1)}, bf16[2048,768]{1,0:T(8,128)(2,...) custom-call(f32[2048,2]{1,0:T(8,128)} %bitcast.152, bf16[2048,2048]{1,0:T(8,128)(2,1)} %all-gather.11.cloned.1.call-done.upstream_ref, ...), custom_call_target="tpu_custom_call" | custom-call | flops 54760833024 | bytes 88080384 | tf_op jit(solution)/shard_map/expert_backward/pallas_call | solution.py:503
  504.7 16.4 %convolution_convert_fusion.5 = bf16[1408,2048]{1,0:T(8,128)(2,1)S(1)} fusion(bf16[2048,1408]{1,0:T(8,128)(2,1)} %get-tuple-element.210, bf16[2048,2048]{1,0:T(8,128)(2,1)} %all-gather.11.cloned.1.call-done.upstream_ref), kind=kOutput, calls=%fused_computation.8 | convolution fusion | flops 11814043648 | bytes 19922944 | tf_op jit(solution)/shard_map/dot_general | solution.py:175
  531.3 19.9 %convolution_convert_fusion.4 = bf16[2048,1536]{1,0:T(8,128)(2,1)} fusion(bf16[2048,2048]{1,0:T(8,128)(2,1)} %all-gather.9.cloned.1.call-done, bf16[2048,1536]{1,0:T(8,128)(2,1)} %get-tuple-element.205), kind=kOutput, calls=%fused_computation.7 | convolution fusion | flops 12888047616 | bytes 20971520 | tf_op jit(solution)/shard_map/dot_general | solution.py:175
  598.5 21.0 %add_convert_fusion = bf16[2048,2048]{1,0:T(8,128)(2,1)} fusion(f32[2048,2048]{1,0:T(8,128)} %fusion.29, bf16[2048,1408]{1,0:T(8,128)(2,1)} %get-tuple-element.210, bf16[1408,512]{1,0:T(8,128)(2,1)} %copy-done.34, bf16[1408,512]{1,0:T(8,128)(2,1)} %copy-done.33, bf16[1408,512]{1,0:T(8,128)(2,1)S(1)} %copy-done.32, bf16[1408,512]{1,0:T(8,128)(2,1)S(1)} %copy-done.30), kind=kOutput, calls=%fused_computation | convolution fusion | flops 11842617344 | bytes 36700160 | tf_op jit(solution)/shard_map/dot_general | solution.py:167
  644.2 10.1 %collective-permute-done.33 = bf16[256,2048]{1,0:T(8,128)(2,1)S(1)} collective-permute-done((bf16[256,2048]{1,0:T(8,128)(2,1)S(1)}, bf16[256,2048]{1,0:T(8,128)(2,1)S(1)}, u32[]{:S(2)}, u32[]{:S(2)}) %collective-permute-start.33) | collective-permute-done | bytes 1048608 | tf_op jit(solution)/shard_map/ppermute | solution.py:40
  679.5 19.2 %attention_backward.1 = bf16[1024,1536]{1,0:T(8,128)(2,1)S(1)} custom-call(s32[1]{0:T(128)S(6)} %copy.135.length_ref, bf16[1024,1536]{1,0:T(8,128)(2,1)} %convolution_convert_fusion.7.query_ref.key_ref.value_ref, bf16[1024,1536]{1,0:T(8,128)(2,1)} %convolution_convert_fusion.7.query_ref.key_ref.value_ref, ...), custom_call_target="tpu_custom_call" | custom-call | flops 6442450944 | bytes 7340032 | tf_op jit(solution)/shard_map/attention_backward/pallas_call | solution.py:423
  726.4 35.3 %collective-permute-done.37 = bf16[128,2048]{1,0:T(8,128)(2,1)} collective-permute-done((bf16[128,2048]{1,0:T(8,128)(2,1)}, bf16[128,2048]{1,0:T(8,128)(2,1)}, u32[]{:S(2)}, u32[]{:S(2)}) %collective-permute-start.37) | collective-permute-done | bytes 524320 | tf_op jit(solution)/shard_map/ppermute | solution.py:40
  769.4 31.7 %convolution_convert_fusion = bf16[2048,2816]{1,0:T(8,128)(2,1)} fusion(bf16[2048,2048]{1,0:T(8,128)(2,1)} %all-gather.9.cloned.1.call-done, bf16[2048,2816]{1,0:T(8,128)(2,1)} %get-tuple-element.248), kind=kOutput, calls=%fused_computation.1 | convolution fusion | flops 23628087296 | bytes 31457280 | tf_op jit(solution)/shard_map/dot_general | solution.py:175
  829.2 28.2 %collective-permute-done.46 = f32[11,2048]{1,0:T(8,128)S(1)} collective-permute-done((f32[11,2048]{1,0:T(8,128)S(1)}, f32[11,2048]{1,0:T(8,128)S(1)}, u32[]{:S(2)}, u32[]{:S(2)}) %collective-permute-start.46) | collective-permute-done | bytes 90144 | tf_op jit(solution)/shard_map/ppermute | solution.py:40
  888.2 50.4 %collective-permute-done.50 = bf16[512,2816]{1,0:T(8,128)(2,1)} collective-permute-done((bf16[512,2816]{1,0:T(8,128)(2,1)}, bf16[512,2816]{1,0:T(8,128)(2,1)}, u32[]{:S(2)}, u32[]{:S(2)}) %collective-permute-start.50) | collective-permute-done | bytes 2883616 | tf_op jit(solution)/shard_map/ppermute | solution.py:40
  (457 shorter events, 402.6 us)
Async XLA Ops:
  7.2 70.5 %all-gather.5.cloned.1.call-start = ((), (), s32[]{:S(2)}) async-start(), calls=%async_computation.10 | async-start | bytes 7077888 | tf_op jit(solution)/shard_map/all_gather | solution.py:144
  48.8 80.0 %all-gather.7.cloned.1.call-start = ((), (), s32[]{:S(2)}) async-start(), calls=%async_computation.11 | async-start | bytes 2359296 | tf_op jit(solution)/shard_map/all_gather | solution.py:559
  109.7 94.8 %all-to-all-start.1 = ((bf16[8,96,1536]{2,1,0:T(8,128)(2,1)}), bf16[8,96,1536]{2,1,0:T(8,128)(2,1)}, u32[]{:S(2)}, u32[]{:S(2)}) async-start(bf16[8,96,1536]{2,1,0:T(8,128)(2,1)} %bitcast.12), calls=%async_computation.1 | async-start | bytes 4718592 | tf_op jit(solution)/shard_map/all_to_all | solution.py:154
  114.6 186.0 %all-gather.9.cloned.1.call-start = ((), (), s32[]{:S(2)}) async-start(), calls=%async_computation.12 | async-start | bytes 9437184 | tf_op jit(solution)/shard_map/all_gather | solution.py:144
  209.9 204.5 %all-gather.11.cloned.1.call-start = ((), (), s32[]{:S(2)}) async-start(), calls=%async_computation.13 | async-start | bytes 9437184 | tf_op jit(solution)/shard_map/all_gather | solution.py:144
  245.1 54.4 %collective-permute-start.19 = (bf16[1,8,96,1536]{3,2,1,0:T(8,128)(2,1)}, bf16[1,8,96,1536]{3,2,1,0:T(8,128)(2,1)}, u32[]{:S(2)}, u32[]{:S(2)}) collective-permute-start(bf16[1,8,96,1536]{3,2,1,0:T(8,128)(2,1)} %bitcast.13), channel_id=1, source_target_pairs={{0,1},{1,0},{2,3},{3,2},{4,5},{5,4},{6,7},{7,6},{8,9},{9,8},{10,11... | collective-permute-start | bytes 7077896 | tf_op jit(solution)/shard_map/ppermute | solution.py:40
  246.1 54.4 %collective-permute-start.20 = (bf16[1,8,96,1536]{3,2,1,0:T(8,128)(2,1)}, bf16[1,8,96,1536]{3,2,1,0:T(8,128)(2,1)}, u32[]{:S(2)}, u32[]{:S(2)}) collective-permute-start(bf16[1,8,96,1536]{3,2,1,0:T(8,128)(2,1)} %bitcast.13), channel_id=1, source_target_pairs={{0,2},{1,3},{2,0},{3,1},{4,6},{5,7},{6,4},{7,5},{8,10},{9,11},{10,... | collective-permute-start | bytes 7077896 | tf_op jit(solution)/shard_map/ppermute | solution.py:40
  257.6 366.6 %reduce-scatter.5.cloned.1.call-start = ((), (), s32[]{:S(2)}) async-start(), calls=%async_computation.14 | async-start | bytes 9437184 | tf_op jit(solution)/shard_map/reduce_scatter | solution.py:148
  270.3 67.0 %collective-permute-start.23 = (bf16[1408,512]{1,0:T(8,128)(2,1)}, bf16[1408,512]{1,0:T(8,128)(2,1)}, u32[]{:S(2)}, u32[]{:S(2)}) collective-permute-start(bf16[1408,512]{1,0:T(8,128)(2,1)} %bitcast.149), channel_id=1, source_target_pairs={{0,1},{1,0},{2,3},{3,2},{4,5},{5,4},{6,7},{7,6},{8,9},{9,8},{10,11... | collective-permute-start | bytes 4325384 | tf_op jit(solution)/shard_map/ppermute | solution.py:40
  271.6 65.6 %collective-permute-start.24 = (bf16[1408,512]{1,0:T(8,128)(2,1)}, bf16[1408,512]{1,0:T(8,128)(2,1)}, u32[]{:S(2)}, u32[]{:S(2)}) collective-permute-start(bf16[1408,512]{1,0:T(8,128)(2,1)} %bitcast.150), channel_id=1, source_target_pairs={{0,2},{1,3},{2,0},{3,1},{4,6},{5,7},{6,4},{7,5},{8,10},{9,11},{10,... | collective-permute-start | bytes 4325384 | tf_op jit(solution)/shard_map/ppermute | solution.py:40
  302.0 50.9 %collective-permute-start.21 = (bf16[1,4,96,1536]{3,2,1,0:T(8,128)(2,1)S(1)}, bf16[1,4,96,1536]{3,2,1,0:T(8,128)(2,1)S(1)}, u32[]{:S(2)}, u32[]{:S(2)}) collective-permute-start(bf16[1,4,96,1536]{3,2,1,0:T(8,128)(2,1)S(1)} %slice.224), channel_id=1, source_target_pairs={{0,1},{1,0},{2,3},{3,2},{4,5},{5,4},{6,7},{7,6},{8,9},{9,8},{10,11... | collective-permute-start | bytes 3538952 | tf_op jit(solution)/shard_map/ppermute | solution.py:40
  304.5 49.4 %collective-permute-start.22 = (bf16[1,4,96,1536]{3,2,1,0:T(8,128)(2,1)S(1)}, bf16[1,4,96,1536]{3,2,1,0:T(8,128)(2,1)S(1)}, u32[]{:S(2)}, u32[]{:S(2)}) collective-permute-start(bf16[1,4,96,1536]{3,2,1,0:T(8,128)(2,1)S(1)} %slice.225), channel_id=1, source_target_pairs={{0,2},{1,3},{2,0},{3,1},{4,6},{5,7},{6,4},{7,5},{8,10},{9,11},{10,... | collective-permute-start | bytes 3538952 | tf_op jit(solution)/shard_map/ppermute | solution.py:40
  527.2 94.9 %all-to-all-start.3 = ((f32[8,2,256]{2,1,0:T(2,128)}), f32[8,2,256]{2,1,0:T(2,128)S(1)}, u32[]{:S(2)}, u32[]{:S(2)}) async-start(f32[8,2,256]{2,1,0:T(2,128)} %bitcast.35), calls=%async_computation.4 | async-start | bytes 32768 | tf_op jit(solution)/shard_map/all_to_all | solution.py:154
  531.2 192.4 %reduce-scatter.7.cloned.1.call-start = ((), (), s32[]{:S(2)}) async-start(), calls=%async_computation.15 | async-start | bytes 9437184 | tf_op jit(solution)/shard_map/reduce_scatter | solution.py:148
  562.6 61.2 %collective-permute-start.32 = (bf16[1408,512]{1,0:T(8,128)(2,1)}, bf16[1408,512]{1,0:T(8,128)(2,1)}, u32[]{:S(2)}, u32[]{:S(2)}) collective-permute-start(bf16[1408,512]{1,0:T(8,128)(2,1)} %pad_maximum_fusion.12), channel_id=1, source_target_pairs={{0,1},{1,0},{2,3},{3,2},{4,5},{5,4},{6,7},{7,6},{8,9},{9,8},{10,11... | collective-permute-start | bytes 4325384 | tf_op jit(solution)/shard_map/ppermute | solution.py:40
  564.7 59.1 %collective-permute-start.31 = (bf16[1408,512]{1,0:T(8,128)(2,1)}, bf16[1408,512]{1,0:T(8,128)(2,1)}, u32[]{:S(2)}, u32[]{:S(2)}) collective-permute-start(bf16[1408,512]{1,0:T(8,128)(2,1)} %pad_maximum_fusion.11), channel_id=1, source_target_pairs={{0,2},{1,3},{2,0},{3,1},{4,6},{5,7},{6,4},{7,5},{8,10},{9,11},{10,... | collective-permute-start | bytes 4325384 | tf_op jit(solution)/shard_map/ppermute | solution.py:40
  623.9 247.1 %reduce-scatter.11.cloned.1.call-start = ((), (), s32[]{:S(2)}) async-start(), calls=%async_computation.17 | async-start | bytes 2359296 | tf_op jit(solution)/shard_map/reduce_scatter | solution.py:148
  674.0 287.8 %reduce-scatter.9.cloned.1.call-start = ((), (), s32[]{:S(2)}) async-start(), calls=%async_computation.16 | async-start | bytes 7077888 | tf_op jit(solution)/shard_map/reduce_scatter | solution.py:148
  698.7 63.0 %collective-permute-start.39 = (bf16[1,8,96,1536]{3,2,0,1:T(8,128)(2,1)}, bf16[1,8,96,1536]{3,2,0,1:T(8,128)(2,1)}, u32[]{:S(2)}, u32[]{:S(2)}) collective-permute-start(bf16[1,8,96,1536]{3,2,0,1:T(8,128)(2,1)} %pad_maximum_fusion.9), channel_id=1, source_target_pairs={{0,2},{1,3},{2,0},{3,1},{4,6},{5,7},{6,4},{7,5},{8,10},{9,11},{10,... | collective-permute-start | bytes 7077896 | tf_op jit(solution)/shard_map/ppermute | solution.py:40
  700.1 61.6 %collective-permute-start.40 = (bf16[1,8,96,1536]{3,2,0,1:T(8,128)(2,1)}, bf16[1,8,96,1536]{3,2,0,1:T(8,128)(2,1)}, u32[]{:S(2)}, u32[]{:S(2)}) collective-permute-start(bf16[1,8,96,1536]{3,2,0,1:T(8,128)(2,1)} %pad_maximum_fusion.10), channel_id=1, source_target_pairs={{0,1},{1,0},{2,3},{3,2},{4,5},{5,4},{6,7},{7,6},{8,9},{9,8},{10,11... | collective-permute-start | bytes 7077896 | tf_op jit(solution)/shard_map/ppermute | solution.py:40
  805.9 77.5 %all-to-all-start.4 = ((bf16[8,96,1536]{2,1,0:T(8,128)(2,1)}), bf16[8,96,1536]{2,1,0:T(8,128)(2,1)}, u32[]{:S(2)}, u32[]{:S(2)}) async-start(bf16[8,96,1536]{2,1,0:T(8,128)(2,1)} %fusion.1), calls=%async_computation.8 | async-start | bytes 4718592 | tf_op jit(solution)/shard_map/all_to_all | solution.py:154
  861.7 76.8 %collective-permute-start.50 = (bf16[512,2816]{1,0:T(8,128)(2,1)}, bf16[512,2816]{1,0:T(8,128)(2,1)}, u32[]{:S(2)}, u32[]{:S(2)}) collective-permute-start(bf16[512,2816]{1,0:T(8,128)(2,1)} %pad_maximum_fusion.6), channel_id=1, source_target_pairs={{0,2},{1,3},{2,0},{3,1},{4,6},{5,7},{6,4},{7,5},{8,10},{9,11},{10,... | collective-permute-start | bytes 8650760 | tf_op jit(solution)/shard_map/ppermute | solution.py:40
  862.9 75.7 %collective-permute-start.51 = (bf16[512,2816]{1,0:T(8,128)(2,1)}, bf16[512,2816]{1,0:T(8,128)(2,1)}, u32[]{:S(2)}, u32[]{:S(2)}) collective-permute-start(bf16[512,2816]{1,0:T(8,128)(2,1)} %pad_maximum_fusion.7), channel_id=1, source_target_pairs={{0,1},{1,0},{2,3},{3,2},{4,5},{5,4},{6,7},{7,6},{8,9},{9,8},{10,11... | collective-permute-start | bytes 8650760 | tf_op jit(solution)/shard_map/ppermute | solution.py:40
  883.4 68.1 %all-to-all-start.5 = ((bf16[4,2,96,1536]{3,2,1,0:T(8,128)(2,1)}), bf16[4,2,96,1536]{3,2,1,0:T(8,128)(2,1)}, u32[]{:S(2)}, u32[]{:S(2)}) async-start(bf16[4,2,96,1536]{3,2,1,0:T(8,128)(2,1)} %bitcast.47), calls=%async_computation.9 | async-start | bytes 4718592 | tf_op jit(solution)/shard_map/all_to_all | solution.py:154
  (130 other events, 2081.4 us)
Sparse Core Ops, SparseCore 0:
  10.3 67.4 all-gather.4
  79.3 29.2 all-gather.6
  210.0 83.3 all-gather.8
  294.9 80.4 all-gather.10
  504.7 88.8 reduce-scatter.4
  624.0 90.3 reduce-scatter.6
  716.6 34.3 reduce-scatter.10
  753.4 73.4 reduce-scatter.8

commit v3 on v2

--- a/solution.py
+++ b/solution.py
@@ -570,6 +570,7 @@
     up_parts = gather_near(expert_up[0])
     shared_blocks = shared_owners(shared_blocks)[None]
     attended, peaks = attention_forward(projected, lengths)
+    attended, up_parts = hold((attended, up_parts))
     middle_parts = scatter_near(scatter_far(times(attended, out_weight).astype(low), 0), 0)
     middle_parts, gate_parts, up_parts, shared_blocks, peaks = hold(
         (middle_parts, gate_parts, up_parts, shared_blocks, peaks)
@@ -660,7 +661,9 @@
     )
     d_w_output = column_scatter(times_first(attended, whole_middle), 1)
     d_normed_rows = times_last(d_projected, in_weights).astype(low)
-    d_normed_rows, d_projected, small_parts = hold((d_normed_rows, d_projected, small_parts))
+    d_normed_rows, d_projected, small_parts, back_s = hold(
+        (d_normed_rows, d_projected, small_parts, back_s)
+    )
     normed_parts = scatter_far(d_normed_rows, 0)
     d_in_weights = column_scatter(times_first(gathered_one, d_projected), 0)
     normed_parts, back_s, d_pre_e, back_down_e = hold(

time: 980 us -> 930 us (0.949)
  waiting for transfers between devices: 324 us -> 265 us
  starting transfers between devices: 89.5 us -> 101 us
    ppermute x52, waiting for transfers between devices: 315 us -> 253 us  [swap(): lax.ppermute(values_in, axis_name, pairs(lax.axis_size(axis_name), bit))]
    all_to_all x6, starting transfers between devices: 27.2 us -> 37 us  [trade(): lax.all_to_all(blocks, axis_name, split_axis=0, concat_axis=0, tiled=True)]
    unnamed x186 -> x190, local copies, waits for them, and re-layouts: 37.5 us -> 34.7 us
  transfers between devices with their start and end apart: 66 -> 66, of which waited for: 36 -> 35; matrix products, arithmetic and copies ran while one was open for 38% -> 41% of each run, Pallas kernels for 4% -> 4%
where the time goes in v3:
time: 930 us; the launch traced here: 922 us
  waiting for transfers between devices  265 us (28%)
  matrix products  213 us (23%)
  Pallas kernels  126 us (14%)
  local copies, waits for them, and re-layouts  117 us (13%)
  starting transfers between devices  101 us (11%)
  other arithmetic  83.7 us (9%)
  between operations  16.5 us (2%)
    ppermute x52, waiting for transfers between devices, swap(): lax.ppermute(values_in, axis_name, pairs(lax.axis_size(axis_name), bit))  253 us
    dot_general x6, matrix products, times(): return jnp.dot(left, right, preferred_element_type=jnp.float32)  98.7 us
    pallas_call x1, Pallas kernels, expert_backward(): pl.pallas_call(expert_backward_kernel, grid=(rows // block,), in_specs=[t...  90.1 us
    dot_general x6, matrix products, times_first(): lax.dot_general(left, right, CONTRACT_FIRST, preferred_element_type=jnp.f...  89.7 us
    ppermute x52, starting transfers between devices, swap(): lax.ppermute(values_in, axis_name, pairs(lax.axis_size(axis_name), bit))  62.2 us
    all_to_all x6, starting transfers between devices, trade(): lax.all_to_all(blocks, axis_name, split_axis=0, concat_axis=0, tiled=True)  37 us
    unnamed x190, local copies, waits for them, and re-layouts  34.7 us
    pallas_call x1, Pallas kernels, attention_backward(): pl.pallas_call(functools.partial(attention_backward_kernel, block_len=blo...  19.2 us
  transfers between devices with their start and end apart: 66, of which 35 were waited for; matrix products, arithmetic and copies ran while one was open for 41% of the time, Pallas kernels for 4%

profile of v3, /device:TPU:0, one launch (start us, length us, event | category | flops | bytes accessed | tf_op | source)
XLA Modules:
  0.0 922.0 jit_solution(6078930553743907438)
XLA Ops:
  21.0 16.0 %collective-permute-done.1 = bf16[256,2048]{1,0:T(8,128)(2,1)} collective-permute-done((bf16[256,2048]{1,0:T(8,128)(2,1)S(1)}, bf16[256,2048]{1,0:T(8,128)(2,1)}, u32[]{:S(2)}, u32[]{:S(2)}) %collective-permute-start.1) | collective-permute-done | bytes 1048608 | tf_op jit(solution)/shard_map/ppermute | solution.py:40
  52.4 16.0 %collective-permute-done.3 = bf16[128,2048]{1,0:T(8,128)(2,1)S(1)} collective-permute-done((bf16[128,2048]{1,0:T(8,128)(2,1)S(1)}, bf16[128,2048]{1,0:T(8,128)(2,1)S(1)}, u32[]{:S(2)}, u32[]{:S(2)}) %collective-permute-start.3) | collective-permute-done | bytes 524320 | tf_op jit(solution)/shard_map/ppermute | solution.py:40
  77.7 12.5 %convolution_convert_fusion.7.query_ref.key_ref.value_ref = bf16[1024,1536]{1,0:T(8,128)(2,1)} fusion(bf16[2048,1536]{1,0:T(8,128)(2,1)} %all-gather.5.cloned.1.call-done, bf16[256,2048]{1,0:T(8,128)(2,1)} %get-tuple-element.338, bf16[256,2048]{1,0:T(8,128)(2,1)} %get-tuple-element.337, bf16[256,2048]{1,0:T(8,128)(2,1)} %get-tuple-element.336, ...), kind=kOutput, calls=%fused_computation.22 | convolution fusion | flops 6460801024 | bytes 13631488 | tf_op jit(solution)/shard_map/dot_general | solution.py:167
  90.2 17.3 %collective-permute-done.4.refs_1_ = bf16[512,1408]{1,0:T(8,128)(2,1)S(1)} collective-permute-done((bf16[512,1408]{1,0:T(8,128)(2,1)}, bf16[512,1408]{1,0:T(8,128)(2,1)S(1)}, u32[]{:S(2)}, u32[]{:S(2)}) %collective-permute-start.4) | collective-permute-done | bytes 1441824 | tf_op jit(solution)/shard_map/ppermute | solution.py:40
  119.4 10.3 %attention_forward.1 = (bf16[1024,512]{1,0:T(8,128)(2,1)S(1)}, f32[4,8,128]{2,1,0:T(8,128)S(1)}) custom-call(s32[1]{0:T(128)S(6)} %copy.135.length_ref, bf16[1024,1536]{1,0:T(8,128)(2,1)S(1)} %copy-done.10, bf16[1024,1536]{1,0:T(8,128)(2,1)S(1)} %copy-done.10, bf16[1024,1536]{1,0:T(8,128)(2,1)S(1)} %copy-done.10), custom_call_target="tpu_custom_call" | custom-call | flops 3221225472 | bytes 4194304 | tf_op jit(solution)/shard_map/attention_forward/pallas_call | solution.py:344
  130.7 10.6 %collective-permute-done.6.refs_6_ = bf16[512,1408]{1,0:T(8,128)(2,1)} collective-permute-done((bf16[512,1408]{1,0:T(8,128)(2,1)}, bf16[512,1408]{1,0:T(8,128)(2,1)}, u32[]{:S(2)}, u32[]{:S(2)}) %collective-permute-start.6) | collective-permute-done | bytes 1441824 | tf_op jit(solution)/shard_map/ppermute | solution.py:40
  169.6 15.8 %collective-permute-done.11 = bf16[256,2048]{1,0:T(8,128)(2,1)} collective-permute-done((bf16[256,2048]{1,0:T(8,128)(2,1)}, bf16[256,2048]{1,0:T(8,128)(2,1)}, u32[]{:S(2)}, u32[]{:S(2)}) %collective-permute-start.11) | collective-permute-done | bytes 1048608 | tf_op jit(solution)/shard_map/ppermute | solution.py:40
  199.7 12.3 %collective-permute-done.12.refs_3_ = bf16[256,1408]{1,0:T(8,128)(2,1)S(1)} collective-permute-done((bf16[256,1408]{1,0:T(8,128)(2,1)S(1)}, bf16[256,1408]{1,0:T(8,128)(2,1)S(1)}, u32[]{:S(2)}, u32[]{:S(2)}) %collective-permute-start.12) | collective-permute-done | bytes 720928 | tf_op jit(solution)/shard_map/ppermute | solution.py:40
  268.7 10.2 %collective-permute-done.19 = bf16[1,8,96,1536]{3,2,1,0:T(8,128)(2,1)} collective-permute-done((bf16[1,8,96,1536]{3,2,1,0:T(8,128)(2,1)}, bf16[1,8,96,1536]{3,2,1,0:T(8,128)(2,1)}, u32[]{:S(2)}, u32[]{:S(2)}) %collective-permute-start.19) | collective-permute-done | bytes 2359328 | tf_op jit(solution)/shard_map/ppermute | solution.py:40
  285.4 32.3 %convolution_convert_fusion.1.refs_0_ = bf16[2048,2816]{1,0:T(8,128)(2,1)} fusion(bf16[2048,2048]{1,0:T(8,128)(2,1)} %all-gather.9.cloned.1.call-done, bf16[2048,2816]{1,0:T(8,128)(2,1)} %join_rows.1.refs_2_), kind=kOutput, calls=%fused_computation.2 | convolution fusion | flops 23628087296 | bytes 31457280 | tf_op jit(solution)/shard_map/dot_general | solution.py:167
  317.7 11.8 %collective-permute-done.21 = bf16[1,4,96,1536]{3,2,1,0:T(8,128)(2,1)S(1)} collective-permute-done((bf16[1,4,96,1536]{3,2,1,0:T(8,128)(2,1)S(1)}, bf16[1,4,96,1536]{3,2,1,0:T(8,128)(2,1)S(1)}, u32[]{:S(2)}, u32[]{:S(2)}) %collective-permute-start.21) | collective-permute-done | bytes 1179680 | tf_op jit(solution)/shard_map/ppermute | solution.py:40
  345.5 19.0 %convolution_convert_fusion.3.refs_1_ = bf16[2048,1536]{1,0:T(8,128)(2,1)} fusion(bf16[2048,2048]{1,0:T(8,128)(2,1)} %all-gather.9.cloned.1.call-done, bf16[2048,1536]{1,0:T(8,128)(2,1)S(1)} %bitcast.133), kind=kOutput, calls=%fused_computation.6 | convolution fusion | flops 12888047616 | bytes 20971520 | tf_op jit(solution)/shard_map/dot_general | solution.py:167
  390.4 90.1 %expert_backward.1 = (bf16[2048,2816]{1,0:T(8,128)(2,1)}, bf16[2048,1536]{1,0:T(8,128)(2,1)}, bf16[2048,1408]{1,0:T(8,128)(2,1)}, bf16[2048,768]{1,0:T(8,128)(2,...) custom-call(f32[2048,2]{1,0:T(8,128)} %bitcast.152, bf16[2048,2048]{1,0:T(8,128)(2,1)} %all-gather.11.cloned.1.call-done.upstream_ref, ...), custom_call_target="tpu_custom_call" | custom-call | flops 54760833024 | bytes 88080384 | tf_op jit(solution)/shard_map/expert_backward/pallas_call | solution.py:503
  480.5 16.4 %convolution_convert_fusion.5 = bf16[1408,2048]{1,0:T(8,128)(2,1)S(1)} fusion(bf16[2048,1408]{1,0:T(8,128)(2,1)} %get-tuple-element.221, bf16[2048,2048]{1,0:T(8,128)(2,1)} %all-gather.11.cloned.1.call-done.upstream_ref), kind=kOutput, calls=%fused_computation.8 | convolution fusion | flops 11814043648 | bytes 19922944 | tf_op jit(solution)/shard_map/dot_general | solution.py:175
  512.3 19.9 %convolution_convert_fusion.4 = bf16[2048,1536]{1,0:T(8,128)(2,1)} fusion(bf16[2048,2048]{1,0:T(8,128)(2,1)} %all-gather.9.cloned.1.call-done, bf16[2048,1536]{1,0:T(8,128)(2,1)} %get-tuple-element.216), kind=kOutput, calls=%fused_computation.7 | convolution fusion | flops 12888047616 | bytes 20971520 | tf_op jit(solution)/shard_map/dot_general | solution.py:175
  569.9 9.6 %fusion.29 = f32[2048,2048]{1,0:T(8,128)} fusion(bf16[2048,768]{1,0:T(8,128)(2,1)S(1)} %copy-done.86, bf16[768,2048]{1,0:T(8,128)(2,1)S(1)} %bitcast.138), kind=kOutput, calls=%fused_computation.185 | convolution fusion | flops 6442450944 | bytes 23068672 | tf_op jit(solution)/shard_map/dot_general | solution.py:167
  579.5 21.1 %add_convert_fusion = bf16[2048,2048]{1,0:T(8,128)(2,1)} fusion(f32[2048,2048]{1,0:T(8,128)} %fusion.29, bf16[2048,1408]{1,0:T(8,128)(2,1)} %get-tuple-element.221, bf16[1408,512]{1,0:T(8,128)(2,1)} %copy-done.35, bf16[1408,512]{1,0:T(8,128)(2,1)} %copy-done.34, bf16[1408,512]{1,0:T(8,128)(2,1)S(1)} %copy-done.33, bf16[1408,512]{1,0:T(8,128)(2,1)S(1)} %copy-done.31), kind=kOutput, calls=%fused_computation | convolution fusion | flops 11842617344 | bytes 36700160 | tf_op jit(solution)/shard_map/dot_general | solution.py:167
  624.9 11.1 %collective-permute-done.33 = bf16[256,2048]{1,0:T(8,128)(2,1)S(1)} collective-permute-done((bf16[256,2048]{1,0:T(8,128)(2,1)S(1)}, bf16[256,2048]{1,0:T(8,128)(2,1)S(1)}, u32[]{:S(2)}, u32[]{:S(2)}) %collective-permute-start.33) | collective-permute-done | bytes 1048608 | tf_op jit(solution)/shard_map/ppermute | solution.py:40
  661.3 19.2 %attention_backward.1 = bf16[1024,1536]{1,0:T(8,128)(2,1)S(1)} custom-call(s32[1]{0:T(128)S(6)} %copy.135.length_ref, bf16[1024,1536]{1,0:T(8,128)(2,1)} %convolution_convert_fusion.7.query_ref.key_ref.value_ref, bf16[1024,1536]{1,0:T(8,128)(2,1)} %convolution_convert_fusion.7.query_ref.key_ref.value_ref, ...), custom_call_target="tpu_custom_call" | custom-call | flops 6442450944 | bytes 7340032 | tf_op jit(solution)/shard_map/attention_backward/pallas_call | solution.py:423
  680.5 11.1 %convolution_convert_fusion.6 = bf16[1024,2048]{1,0:T(8,128)(2,1)} fusion(bf16[1024,1536]{1,0:T(8,128)(2,1)S(1)} %attention_backward.1, bf16[2048,1536]{1,0:T(8,128)(2,1)} %all-gather.5.cloned.1.call-done), kind=kOutput, calls=%fused_computation.21 | convolution fusion | flops 6444548096 | bytes 13631488 | tf_op jit(solution)/shard_map/dot_general | solution.py:171
  721.8 31.7 %convolution_convert_fusion = bf16[2048,2816]{1,0:T(8,128)(2,1)} fusion(bf16[2048,2048]{1,0:T(8,128)(2,1)} %all-gather.9.cloned.1.call-done, bf16[2048,2816]{1,0:T(8,128)(2,1)} %get-tuple-element.262), kind=kOutput, calls=%fused_computation.1 | convolution fusion | flops 23628087296 | bytes 31457280 | tf_op jit(solution)/shard_map/dot_general | solution.py:175
  779.9 28.2 %collective-permute-done.46 = f32[11,2048]{1,0:T(8,128)S(1)} collective-permute-done((f32[11,2048]{1,0:T(8,128)S(1)}, f32[11,2048]{1,0:T(8,128)S(1)}, u32[]{:S(2)}, u32[]{:S(2)}) %collective-permute-start.46) | collective-permute-done | bytes 90144 | tf_op jit(solution)/shard_map/ppermute | solution.py:40
  822.6 15.7 %collective-permute-done.48 = f32[11,2048]{1,0:T(8,128)S(1)} collective-permute-done((f32[11,2048]{1,0:T(8,128)S(1)}, f32[11,2048]{1,0:T(8,128)S(1)}, u32[]{:S(2)}, u32[]{:S(2)}) %collective-permute-start.48) | collective-permute-done | bytes 90144 | tf_op jit(solution)/shard_map/ppermute | solution.py:40
  860.5 28.8 %collective-permute-done.50 = bf16[512,2816]{1,0:T(8,128)(2,1)} collective-permute-done((bf16[512,2816]{1,0:T(8,128)(2,1)}, bf16[512,2816]{1,0:T(8,128)(2,1)}, u32[]{:S(2)}, u32[]{:S(2)}) %collective-permute-start.50) | collective-permute-done | bytes 2883616 | tf_op jit(solution)/shard_map/ppermute | solution.py:40
  (461 shorter events, 418.6 us)
Async XLA Ops:
  7.2 70.5 %all-gather.5.cloned.1.call-start = ((), (), s32[]{:S(2)}) async-start(), calls=%async_computation.10 | async-start | bytes 7077888 | tf_op jit(solution)/shard_map/all_gather | solution.py:144
  48.8 93.2 %all-gather.7.cloned.1.call-start = ((), (), s32[]{:S(2)}) async-start(), calls=%async_computation.11 | async-start | bytes 2359296 | tf_op jit(solution)/shard_map/all_gather | solution.py:559
  111.7 75.7 %all-to-all-start.1 = ((bf16[8,96,1536]{2,1,0:T(8,128)(2,1)}), bf16[8,96,1536]{2,1,0:T(8,128)(2,1)}, u32[]{:S(2)}, u32[]{:S(2)}) async-start(bf16[8,96,1536]{2,1,0:T(8,128)(2,1)} %bitcast.12), calls=%async_computation.1 | async-start | bytes 4718592 | tf_op jit(solution)/shard_map/all_to_all | solution.py:154
  116.6 163.4 %all-gather.9.cloned.1.call-start = ((), (), s32[]{:S(2)}) async-start(), calls=%async_computation.12 | async-start | bytes 9437184 | tf_op jit(solution)/shard_map/all_gather | solution.py:144
  192.8 197.5 %all-gather.11.cloned.1.call-start = ((), (), s32[]{:S(2)}) async-start(), calls=%async_computation.13 | async-start | bytes 9437184 | tf_op jit(solution)/shard_map/all_gather | solution.py:144
  224.4 54.4 %collective-permute-start.19 = (bf16[1,8,96,1536]{3,2,1,0:T(8,128)(2,1)}, bf16[1,8,96,1536]{3,2,1,0:T(8,128)(2,1)}, u32[]{:S(2)}, u32[]{:S(2)}) collective-permute-start(bf16[1,8,96,1536]{3,2,1,0:T(8,128)(2,1)} %bitcast.13), channel_id=1, source_target_pairs={{0,1},{1,0},{2,3},{3,2},{4,5},{5,4},{6,7},{7,6},{8,9},{9,8},{10,11... | collective-permute-start | bytes 7077896 | tf_op jit(solution)/shard_map/ppermute | solution.py:40
  225.6 54.4 %collective-permute-start.20 = (bf16[1,8,96,1536]{3,2,1,0:T(8,128)(2,1)}, bf16[1,8,96,1536]{3,2,1,0:T(8,128)(2,1)}, u32[]{:S(2)}, u32[]{:S(2)}) collective-permute-start(bf16[1,8,96,1536]{3,2,1,0:T(8,128)(2,1)} %bitcast.13), channel_id=1, source_target_pairs={{0,2},{1,3},{2,0},{3,1},{4,6},{5,7},{6,4},{7,5},{8,10},{9,11},{10,... | collective-permute-start | bytes 7077896 | tf_op jit(solution)/shard_map/ppermute | solution.py:40
  241.0 364.8 %reduce-scatter.5.cloned.1.call-start = ((), (), s32[]{:S(2)}) async-start(), calls=%async_computation.14 | async-start | bytes 9437184 | tf_op jit(solution)/shard_map/reduce_scatter | solution.py:148
  254.7 63.0 %collective-permute-start.23 = (bf16[1408,512]{1,0:T(8,128)(2,1)}, bf16[1408,512]{1,0:T(8,128)(2,1)}, u32[]{:S(2)}, u32[]{:S(2)}) collective-permute-start(bf16[1408,512]{1,0:T(8,128)(2,1)} %bitcast.149), channel_id=1, source_target_pairs={{0,1},{1,0},{2,3},{3,2},{4,5},{5,4},{6,7},{7,6},{8,9},{9,8},{10,11... | collective-permute-start | bytes 4325384 | tf_op jit(solution)/shard_map/ppermute | solution.py:40
  256.2 61.5 %collective-permute-start.24 = (bf16[1408,512]{1,0:T(8,128)(2,1)}, bf16[1408,512]{1,0:T(8,128)(2,1)}, u32[]{:S(2)}, u32[]{:S(2)}) collective-permute-start(bf16[1408,512]{1,0:T(8,128)(2,1)} %bitcast.150), channel_id=1, source_target_pairs={{0,2},{1,3},{2,0},{3,1},{4,6},{5,7},{6,4},{7,5},{8,10},{9,11},{10,... | collective-permute-start | bytes 4325384 | tf_op jit(solution)/shard_map/ppermute | solution.py:40
  281.4 48.1 %collective-permute-start.21 = (bf16[1,4,96,1536]{3,2,1,0:T(8,128)(2,1)S(1)}, bf16[1,4,96,1536]{3,2,1,0:T(8,128)(2,1)S(1)}, u32[]{:S(2)}, u32[]{:S(2)}) collective-permute-start(bf16[1,4,96,1536]{3,2,1,0:T(8,128)(2,1)S(1)} %slice.224), channel_id=1, source_target_pairs={{0,1},{1,0},{2,3},{3,2},{4,5},{5,4},{6,7},{7,6},{8,9},{9,8},{10,11... | collective-permute-start | bytes 3538952 | tf_op jit(solution)/shard_map/ppermute | solution.py:40
  331.5 49.3 %collective-permute-start.25 = (bf16[704,512]{1,0:T(8,128)(2,1)}, bf16[704,512]{1,0:T(8,128)(2,1)}, u32[]{:S(2)}, u32[]{:S(2)}) collective-permute-start(bf16[704,512]{1,0:T(8,128)(2,1)} %slice.227), channel_id=1, source_target_pairs={{0,1},{1,0},{2,3},{3,2},{4,5},{5,4},{6,7},{7,6},{8,9},{9,8},{10,11... | collective-permute-start | bytes 2162696 | tf_op jit(solution)/shard_map/ppermute | solution.py:40
  334.0 48.0 %collective-permute-start.26 = (bf16[704,512]{1,0:T(8,128)(2,1)}, bf16[704,512]{1,0:T(8,128)(2,1)S(1)}, u32[]{:S(2)}, u32[]{:S(2)}) collective-permute-start(bf16[704,512]{1,0:T(8,128)(2,1)} %slice.228), channel_id=1, source_target_pairs={{0,2},{1,3},{2,0},{3,1},{4,6},{5,7},{6,4},{7,5},{8,10},{9,11},{10,... | collective-permute-start | bytes 2162696 | tf_op jit(solution)/shard_map/ppermute | solution.py:40
  502.7 100.5 %all-to-all-start.3 = ((f32[8,2,256]{2,1,0:T(2,128)}), f32[8,2,256]{2,1,0:T(2,128)S(1)}, u32[]{:S(2)}, u32[]{:S(2)}) async-start(f32[8,2,256]{2,1,0:T(2,128)} %bitcast.35), calls=%async_computation.4 | async-start | bytes 32768 | tf_op jit(solution)/shard_map/all_to_all | solution.py:154
  512.2 182.8 %reduce-scatter.7.cloned.1.call-start = ((), (), s32[]{:S(2)}) async-start(), calls=%async_computation.15 | async-start | bytes 9437184 | tf_op jit(solution)/shard_map/reduce_scatter | solution.py:148
  543.7 61.7 %collective-permute-start.32 = (bf16[1408,512]{1,0:T(8,128)(2,1)}, bf16[1408,512]{1,0:T(8,128)(2,1)}, u32[]{:S(2)}, u32[]{:S(2)}) collective-permute-start(bf16[1408,512]{1,0:T(8,128)(2,1)} %pad_maximum_fusion.12), channel_id=1, source_target_pairs={{0,1},{1,0},{2,3},{3,2},{4,5},{5,4},{6,7},{7,6},{8,9},{9,8},{10,11... | collective-permute-start | bytes 4325384 | tf_op jit(solution)/shard_map/ppermute | solution.py:40
  546.2 59.2 %collective-permute-start.31 = (bf16[1408,512]{1,0:T(8,128)(2,1)}, bf16[1408,512]{1,0:T(8,128)(2,1)}, u32[]{:S(2)}, u32[]{:S(2)}) collective-permute-start(bf16[1408,512]{1,0:T(8,128)(2,1)} %pad_maximum_fusion.11), channel_id=1, source_target_pairs={{0,2},{1,3},{2,0},{3,1},{4,6},{5,7},{6,4},{7,5},{8,10},{9,11},{10,... | collective-permute-start | bytes 4325384 | tf_op jit(solution)/shard_map/ppermute | solution.py:40
  605.4 215.3 %reduce-scatter.11.cloned.1.call-start = ((), (), s32[]{:S(2)}) async-start(), calls=%async_computation.17 | async-start | bytes 2359296 | tf_op jit(solution)/shard_map/reduce_scatter | solution.py:148
  649.8 50.7 %collective-permute-start.37 = (bf16[1,8,96,1536]{3,2,0,1:T(8,128)(2,1)}, bf16[1,8,96,1536]{3,2,0,1:T(8,128)(2,1)}, u32[]{:S(2)}, u32[]{:S(2)}) collective-permute-start(bf16[1,8,96,1536]{3,2,0,1:T(8,128)(2,1)} %pad_maximum_fusion.9), channel_id=1, source_target_pairs={{0,2},{1,3},{2,0},{3,1},{4,6},{5,7},{6,4},{7,5},{8,10},{9,11},{10,... | collective-permute-start | bytes 7077896 | tf_op jit(solution)/shard_map/ppermute | solution.py:40
  650.5 50.2 %collective-permute-start.38 = (bf16[1,8,96,1536]{3,2,0,1:T(8,128)(2,1)}, bf16[1,8,96,1536]{3,2,0,1:T(8,128)(2,1)}, u32[]{:S(2)}, u32[]{:S(2)}) collective-permute-start(bf16[1,8,96,1536]{3,2,0,1:T(8,128)(2,1)} %pad_maximum_fusion.10), channel_id=1, source_target_pairs={{0,1},{1,0},{2,3},{3,2},{4,5},{5,4},{6,7},{7,6},{8,9},{9,8},{10,11... | collective-permute-start | bytes 7077896 | tf_op jit(solution)/shard_map/ppermute | solution.py:40
  656.5 256.1 %reduce-scatter.9.cloned.1.call-start = ((), (), s32[]{:S(2)}) async-start(), calls=%async_computation.16 | async-start | bytes 7077888 | tf_op jit(solution)/shard_map/reduce_scatter | solution.py:148
  758.3 97.5 %all-to-all-start.4 = ((bf16[8,96,1536]{2,1,0:T(8,128)(2,1)}), bf16[8,96,1536]{2,1,0:T(8,128)(2,1)}, u32[]{:S(2)}, u32[]{:S(2)}) async-start(bf16[8,96,1536]{2,1,0:T(8,128)(2,1)} %fusion.1), calls=%async_computation.8 | async-start | bytes 4718592 | tf_op jit(solution)/shard_map/all_to_all | solution.py:154
  812.5 76.8 %collective-permute-start.50 = (bf16[512,2816]{1,0:T(8,128)(2,1)}, bf16[512,2816]{1,0:T(8,128)(2,1)}, u32[]{:S(2)}, u32[]{:S(2)}) collective-permute-start(bf16[512,2816]{1,0:T(8,128)(2,1)} %pad_maximum_fusion.6), channel_id=1, source_target_pairs={{0,2},{1,3},{2,0},{3,1},{4,6},{5,7},{6,4},{7,5},{8,10},{9,11},{10,... | collective-permute-start | bytes 8650760 | tf_op jit(solution)/shard_map/ppermute | solution.py:40
  813.5 75.8 %collective-permute-start.51 = (bf16[512,2816]{1,0:T(8,128)(2,1)}, bf16[512,2816]{1,0:T(8,128)(2,1)}, u32[]{:S(2)}, u32[]{:S(2)}) collective-permute-start(bf16[512,2816]{1,0:T(8,128)(2,1)} %pad_maximum_fusion.7), channel_id=1, source_target_pairs={{0,1},{1,0},{2,3},{3,2},{4,5},{5,4},{6,7},{7,6},{8,9},{9,8},{10,11... | collective-permute-start | bytes 8650760 | tf_op jit(solution)/shard_map/ppermute | solution.py:40
  (132 other events, 1931.1 us)
Sparse Core Ops, SparseCore 0:
  10.3 67.4 all-gather.4
  79.3 29.2 all-gather.6
  193.0 86.5 all-gather.8
  281.0 80.4 all-gather.10
  480.6 94.0 reduce-scatter.4
  605.6 89.3 reduce-scatter.6
  697.3 34.5 reduce-scatter.10
  734.2 98.2 reduce-scatter.8
